TPU v7x, 32 devices: a whole 2x2x4 slice. The times are simulated.
32 devices in a mesh: dp: 8 (over y, x, core), tensor: 4 (over z).
Axes of the slice: x: 2, y: 2, z: 4, core: 2. Of those that a mesh axis runs over, the one named last changes fastest.
Arguments:
- tokens: bfloat16 [16384, 768], P(('dp', 'tensor')), may hold values from -6 to 6
- qkv_weight: bfloat16 [3, 768, 768], P(None, None, 'tensor'), may hold values from -0.21875 to 0.21875
- rel_weight: bfloat16 [768, 64], P('tensor'), may hold values from -0.75 to 0.75
- out_weight: bfloat16 [768, 768], P('tensor'), may hold values from -1.75 to 1.75
- ffn_in_weight: bfloat16 [768, 3072], P(None, 'tensor'), may hold values from -0.21875 to 0.21875
- ffn_in_bias: float32 [3072], P('tensor'), may hold values from -3 to 3
- ffn_out_weight: bfloat16 [3072, 768], P('tensor'), may hold values from -0.109375 to 0.109375
- norm_gains: float32 [2, 768], replicated, may hold values from 0.5 to 1.5
- norm_biases: float32 [2, 768], replicated, may hold values from -3 to 3
- page_lengths: int32 [32], P('dp'), may hold values from 40 to 512, as said below
- boxes: int32 [2, 16384], P(None, 'dp'), may hold values from 0 to 1000
- out_grad: bfloat16 [16384, 768], P(('dp', 'tensor')), may hold values from -6 to 6
Outputs:
- layer_out: bfloat16 [16384, 768], P(('dp', 'tensor'))
- tokens_grad: bfloat16 [16384, 768], P(('dp', 'tensor'))
- qkv_grad: float32 [3, 768, 768], P(None, None, 'tensor')
- rel_grad: float32 [768, 64], P('tensor')
- out_weight_grad: float32 [768, 768], P('tensor')
- ffn_in_grad: float32 [768, 3072], P(None, 'tensor')
- ffn_bias_grad: float32 [3072], P('tensor')
- ffn_out_grad: float32 [3072, 768], P('tensor')
- gains_grad: float32 [2, 768], replicated
- biases_grad: float32 [2, 768], replicated
- masked_rms: float32 [3], replicated
Inputs may be any that keep to these rules, and one draw needn't show every extreme that they name: `page_lengths`: lengths of 40 and of 512 occur in every draw.
All inputs are finite; a program needn't handle non-finite values.
Results may differ from a plain program's by a relative error of at most 0.018.
Values may be sent and summed in bfloat16 or wider, within the bound.
A program may use at most 128 MiB of HBM per device.

v0:
```python
from functools import partial
import math

import jax
import jax.numpy as jnp
from jax import lax
from jax.sharding import PartitionSpec as P

HEAD_DIM = 64
PAGE = 512
FREQ = 16
POS = 64


norm_epsilon = 1e-05
score_scale = 0.125
masked_score = -1000000000.0


def position_features(boxes_rows):
    orders = jnp.arange(FREQ, dtype=jnp.float32)
    rates = 0.5 * jnp.exp(orders * (-math.log(100.0) / FREQ))
    angles = boxes_rows.astype(jnp.float32)[:, None, :] * rates[None, :, None]
    angles = angles.reshape(2 * FREQ, boxes_rows.shape[1])
    return jnp.concatenate([jnp.cos(angles), jnp.sin(angles)], 0).T


def rotate(coeffs, cos_part, sin_part):
    halfway = coeffs.shape[-1] // 2
    first, second = (coeffs[..., :halfway], coeffs[..., halfway:])
    return jnp.concatenate(
        [first * sin_part + second * cos_part, second * sin_part - first * cos_part], -1
    )


def rotate_back(grad_turned, cos_part, sin_part):
    halfway = grad_turned.shape[-1] // 2
    first, second = (grad_turned[..., :halfway], grad_turned[..., halfway:])
    return jnp.concatenate(
        [first * sin_part - second * cos_part, first * cos_part + second * sin_part], -1
    )


def layer_norm(values, gain, shift):
    average = jnp.mean(values, -1, keepdims=True)
    centred = values - average
    spread = jnp.mean(centred * centred, -1, keepdims=True)
    return centred * lax.rsqrt(spread + norm_epsilon) * gain + shift


def page_scores(queries_page, keys_page, key_valid):
    scores = (
        jnp.einsum("qhe,khe->hqk", queries_page, keys_page, preferred_element_type=jnp.float32)
        * score_scale
    )
    return jnp.where(key_valid[None, None, :], scores, masked_score)


def page_forward(member):
    queries_page, keys_page, values_page, key_valid = member
    scores = page_scores(queries_page, keys_page, key_valid)
    highest_score = jnp.max(scores, -1, keepdims=True)
    raised = jnp.exp(scores - highest_score)
    row_totals = jnp.sum(raised, -1, keepdims=True)
    weights = (raised / row_totals).astype(jnp.bfloat16)
    attended = jnp.einsum("hqk,khd->qhd", weights, values_page, preferred_element_type=jnp.float32)
    return (attended, (highest_score + jnp.log(row_totals))[..., 0])


def page_backward(member):
    queries_page, keys_page, values_page, key_valid, log_totals, grad_attended = member
    scores = page_scores(queries_page, keys_page, key_valid)
    probs = jnp.exp(scores - log_totals[..., None])
    grad_weights = jnp.einsum(
        "qhd,khd->hqk", grad_attended, values_page, preferred_element_type=jnp.float32
    )
    inner = jnp.sum(probs * grad_weights, -1, keepdims=True)
    grad_scores = (probs * (grad_weights - inner)).astype(jnp.bfloat16)
    grad_queries = (
        jnp.einsum("hqk,khe->qhe", grad_scores, keys_page, preferred_element_type=jnp.float32)
        * score_scale
    )
    grad_keys = (
        jnp.einsum("hqk,qhe->khe", grad_scores, queries_page, preferred_element_type=jnp.float32)
        * score_scale
    )
    grad_values = jnp.einsum(
        "hqk,qhd->khd",
        probs.astype(jnp.bfloat16),
        grad_attended,
        preferred_element_type=jnp.float32,
    )
    return (grad_queries, grad_keys[..., :HEAD_DIM], grad_values)


def per_device(
    tokens,
    qkv_weight,
    rel_weight,
    out_weight,
    ffn_in_weight,
    ffn_in_bias,
    ffn_out_weight,
    norm_gains,
    norm_biases,
    page_lengths,
    boxes,
    out_grad,
):
    rows_dev = tokens.shape[0]
    width = tokens.shape[1]
    group_rows = boxes.shape[1]
    pages_here = page_lengths.shape[0]
    head_cols = out_weight.shape[0]
    heads_here = head_cols // HEAD_DIM
    features = position_features(boxes)
    halfway = POS // 2
    cos_part = features[:, None, :halfway]
    sin_part = features[:, None, halfway:]
    key_valid = jnp.arange(PAGE, dtype=jnp.int32)[None, :] < page_lengths[:, None]
    row_place = lax.axis_index("tensor") * rows_dev + jnp.arange(rows_dev, dtype=jnp.int32)
    page_of_row = row_place // PAGE
    row_limit = jnp.sum(
        jnp.where(
            page_of_row[:, None] == jnp.arange(pages_here, dtype=jnp.int32)[None, :],
            page_lengths[None, :],
            0,
        ),
        1,
    )
    valid_rows = (row_place % PAGE < row_limit).astype(jnp.float32)[:, None]
    whole_tokens = lax.all_gather(tokens, "tensor", axis=0, tiled=True)
    projected = jnp.einsum(
        "td,cdh->cth", whole_tokens, qkv_weight, preferred_element_type=jnp.float32
    ).astype(jnp.bfloat16)
    queries = projected[0].reshape(group_rows, heads_here, HEAD_DIM)
    keys_head = projected[1].reshape(group_rows, heads_here, HEAD_DIM)
    values_head = projected[2].reshape(group_rows, heads_here, HEAD_DIM)
    relation = rel_weight.reshape(heads_here, HEAD_DIM, POS)
    coeffs = jnp.einsum("thd,hdp->thp", queries, relation, preferred_element_type=jnp.float32)
    turned = rotate(coeffs, cos_part, sin_part).astype(jnp.bfloat16)
    placed = jnp.broadcast_to(
        features.astype(jnp.bfloat16)[:, None, :], (group_rows, heads_here, POS)
    )
    query_full = jnp.concatenate([queries, turned], -1)
    key_full = jnp.concatenate([keys_head, placed], -1)

    def to_pages(array):
        return array.reshape((pages_here, PAGE) + array.shape[1:])

    paged = (to_pages(query_full), to_pages(key_full), to_pages(values_head), key_valid)
    attended, log_totals = lax.map(page_forward, paged)
    attended_low = attended.reshape(group_rows, head_cols).astype(jnp.bfloat16)
    attn_out = lax.psum_scatter(
        jnp.dot(attended_low, out_weight, preferred_element_type=jnp.float32).astype(jnp.bfloat16),
        "tensor",
        scatter_dimension=0,
        tiled=True,
    ).astype(jnp.float32)
    tokens_value = tokens.astype(jnp.float32)
    residual_one = tokens_value + attn_out
    normed, norm_back_one = jax.vjp(layer_norm, residual_one, norm_gains[0], norm_biases[0])
    whole_normed = lax.all_gather(normed.astype(jnp.bfloat16), "tensor", axis=0, tiled=True)
    hidden_pre = (
        jnp.dot(whole_normed, ffn_in_weight, preferred_element_type=jnp.float32) + ffn_in_bias
    )
    hidden_act, gelu_back = jax.vjp(partial(jax.nn.gelu, approximate=False), hidden_pre)
    hidden_low = hidden_act.astype(jnp.bfloat16)
    ffn_out = lax.psum_scatter(
        jnp.dot(
            lax.slice_in_dim(hidden_low, 0, lax.axis_size("tensor") * rows_dev, axis=0),
            ffn_out_weight,
            preferred_element_type=jnp.float32,
        ).astype(jnp.bfloat16),
        "tensor",
        scatter_dimension=0,
        tiled=True,
    ).astype(jnp.float32)
    result, norm_back_two = jax.vjp(layer_norm, normed + ffn_out, norm_gains[1], norm_biases[1])
    stats = jnp.stack(
        [
            jnp.sum(valid_rows * tokens_value * tokens_value),
            jnp.sum(valid_rows * attn_out * attn_out),
            jnp.sum(valid_rows * ffn_out * ffn_out),
            jnp.sum(valid_rows) * width,
        ]
    )
    stats_total = lax.psum(stats, ("dp", "tensor"))
    grad_two, gain_two, shift_two = norm_back_two(out_grad.astype(jnp.float32))
    whole_ffn_grad = lax.all_gather(grad_two.astype(jnp.bfloat16), "tensor", axis=0, tiled=True)
    ffn_out_grad = jnp.einsum(
        "tf,td->fd", hidden_low, whole_ffn_grad, preferred_element_type=jnp.float32
    )
    grad_hidden = jnp.einsum(
        "td,fd->tf", whole_ffn_grad, ffn_out_weight, preferred_element_type=jnp.float32
    )
    grad_pre = gelu_back(grad_hidden)[0].astype(jnp.bfloat16)
    ffn_bias_grad = jnp.sum(grad_pre.astype(jnp.float32), 0)
    ffn_in_grad = jnp.einsum(
        "td,tf->df", whole_normed, grad_pre, preferred_element_type=jnp.float32
    )
    grad_normed = grad_two + lax.psum_scatter(
        jnp.einsum("tf,df->td", grad_pre, ffn_in_weight, preferred_element_type=jnp.float32).astype(
            jnp.bfloat16
        ),
        "tensor",
        scatter_dimension=0,
        tiled=True,
    ).astype(jnp.float32)
    grad_one, gain_one, shift_one = norm_back_one(grad_normed)
    grad_one_low = grad_one.astype(jnp.bfloat16)
    whole_attn_grad = lax.all_gather(grad_one_low, "tensor", axis=0, tiled=True)
    out_weight_grad = jnp.einsum(
        "th,td->hd", attended_low, whole_attn_grad, preferred_element_type=jnp.float32
    )
    grad_attended = jnp.einsum(
        "td,hd->th", whole_attn_grad, out_weight, preferred_element_type=jnp.float32
    ).astype(jnp.bfloat16)
    grad_attended = grad_attended.reshape(group_rows, heads_here, HEAD_DIM)
    grad_query_full, grad_keys, grad_values = lax.map(
        page_backward, paged + (log_totals, to_pages(grad_attended))
    )
    grad_query_full = grad_query_full.reshape(group_rows, heads_here, HEAD_DIM + POS)
    grad_turned = grad_query_full[..., HEAD_DIM:].astype(jnp.bfloat16)
    grad_coeffs = rotate_back(grad_turned.astype(jnp.float32), cos_part, sin_part).astype(
        jnp.bfloat16
    )
    grad_queries = (
        grad_query_full[..., :HEAD_DIM]
        + jnp.einsum("thp,hdp->thd", grad_coeffs, relation, preferred_element_type=jnp.float32)
    ).astype(jnp.bfloat16)
    rel_grad = jnp.einsum(
        "thd,thp->hdp", queries, grad_coeffs, preferred_element_type=jnp.float32
    ).reshape(head_cols, POS)
    grad_projected = jnp.stack(
        [
            grad_queries.reshape(group_rows, head_cols),
            grad_keys.reshape(group_rows, head_cols).astype(jnp.bfloat16),
            grad_values.reshape(group_rows, head_cols).astype(jnp.bfloat16),
        ]
    )
    qkv_grad = jnp.einsum(
        "td,cth->cdh", whole_tokens, grad_projected, preferred_element_type=jnp.float32
    )
    tokens_grad = (
        grad_one
        + lax.psum_scatter(
            jnp.einsum(
                "cth,cdh->td", grad_projected, qkv_weight, preferred_element_type=jnp.float32
            ).astype(jnp.bfloat16),
            "tensor",
            scatter_dimension=0,
            tiled=True,
        ).astype(jnp.float32)
    ).astype(jnp.bfloat16)
    qkv_grad, rel_grad, out_weight_grad, ffn_in_grad, ffn_bias_grad, ffn_out_grad = lax.psum(
        (qkv_grad, rel_grad, out_weight_grad, ffn_in_grad, ffn_bias_grad, ffn_out_grad), "dp"
    )
    gains_local = jnp.stack([gain_one, gain_two])
    shifts_local = jnp.stack([shift_one, shift_two])
    gains_grad, biases_grad = lax.psum((gains_local, shifts_local), ("dp", "tensor"))
    root_means = jnp.sqrt(stats_total[:3] / stats_total[3])
    return (
        result.astype(jnp.bfloat16),
        tokens_grad,
        qkv_grad,
        rel_grad,
        out_weight_grad,
        ffn_in_grad,
        ffn_bias_grad,
        ffn_out_grad,
        gains_grad,
        biases_grad,
        root_means,
    )


def solution(mesh):
    return jax.shard_map(
        per_device,
        mesh=mesh,
        in_specs=(
            P(("dp", "tensor"), None),
            P(None, None, "tensor"),
            P("tensor", None),
            P("tensor", None),
            P(None, "tensor"),
            P("tensor"),
            P("tensor", None),
            P(),
            P(),
            P("dp"),
            P(None, "dp"),
            P(("dp", "tensor"), None),
        ),
        out_specs=(
            P(("dp", "tensor"), None),
            P(("dp", "tensor"), None),
            P(None, None, "tensor"),
            P("tensor", None),
            P("tensor", None),
            P(None, "tensor"),
            P("tensor"),
            P("tensor", None),
            P(),
            P(),
            P(),
        ),
        check_vma=False,
    )
```

profile of v0, /device:TPU:0, one launch (start us, length us, event | category | flops | bytes accessed | tf_op | source)
XLA Modules:
  0.0 907.3 jit_solution(6940289307698425460)
XLA Ops:
  14.0 61.9 %all-gather.5.cloned.1.call-done = bf16[2048,768]{1,0:T(8,128)(2,1)} async-done(((bf16[512,768]{1,0:T(8,128)(2,1)}), bf16[2048,768]{1,0:T(8,128)(2,1)}) %all-gather.5.cloned.1.call-update) | async-done | bytes 3145744 | tf_op jit(solution)/shard_map/all_gather | solution.py:132
  75.8 3.9 fusion.60
  100.1 5.9 pad_maximum_fusion.1
  106.1 19.3 %while.26 = (s32[]{:T(128)}, bf16[4,512,3,64]{1,3,2,0:T(8,128)(2,1)S(1)}, f32[4,3,512]{2,1,0:T(4,128)}, bf16[4,512,3,64]{1,3,2,0:T(8,128)(2,1)}, pred[4,512]{1,0...) while((s32[]{:T(128)}, ...), condition=%wide.region_3.4_spmd, body=%wide.region_0.3_spmd.sunk | while | flops 311425536 | bytes 10873945 | solution.py:152
  131.2 57.8 %reduce-scatter.5.cloned.1.call-done = bf16[512,768]{1,0:T(8,128)(2,1)} async-done(((bf16[2048,768]{1,0:T(8,128)(2,1)}), bf16[512,768]{1,0:T(8,128)(2,1)}) %reduce-scatter.5.cloned.1.call-update) | async-done | bytes 786448 | tf_op jit(solution)/shard_map/reduce_scatter | solution.py:154
  193.4 63.6 %all-gather.7.cloned.1.call-done = bf16[2048,768]{1,0:T(8,128)(2,1)} async-done(((bf16[512,768]{1,0:T(8,128)(2,1)}), bf16[2048,768]{1,0:T(8,128)(2,1)}) %all-gather.7.cloned.1.call-update) | async-done | bytes 3145744 | tf_op jit(solution)/shard_map/all_gather | solution.py:163
  257.0 18.7 %multiply_convert_fusion.1 = (bf16[2048,768]{1,0:T(8,128)(2,1)S(1)}, f32[2048,768]{1,0:T(8,128)}, f32[2048,768]{1,0:T(8,128)}) fusion(f32[768]{0:T(1024)S(1)} %copy-done.51, bf16[2048,768]{1,0:T(8,128)(2,1)} %all-gather.7.cloned.1.call-done, bf16[768,768]{1,0:T(8,128)(2,1)S(1)} %copy-done), kind=kOutput, calls=%fused_computation.61 | convolution fusion | flops 2519728128 | bytes 20057088 | tf_op jit(solution)/shard_map/dot_general | solution.py:165
  277.4 4.0 convolution_convert_fusion.1
  281.4 59.0 %reduce-scatter.7.cloned.1.call-done = bf16[512,768]{1,0:T(8,128)(2,1)} async-done(((bf16[2048,768]{1,0:T(8,128)(2,1)}), bf16[512,768]{1,0:T(8,128)(2,1)}) %reduce-scatter.7.cloned.1.call-update) | async-done | bytes 786448 | tf_op jit(solution)/shard_map/reduce_scatter | solution.py:169
  349.1 63.6 %all-gather.9.cloned.1.call-done = bf16[2048,768]{1,0:T(8,128)(2,1)} async-done(((bf16[512,768]{1,0:T(8,128)(2,1)}), bf16[2048,768]{1,0:T(8,128)(2,1)}) %all-gather.9.cloned.1.call-update) | async-done | bytes 3145744 | tf_op jit(solution)/shard_map/all_gather | solution.py:190
  412.7 11.1 %convert_reduce_fusion = (f32[768]{0:T(1024)}, bf16[2048,768]{1,0:T(8,128)(2,1)S(1)}) fusion(f32[2048,768]{1,0:T(8,128)} %get-tuple-element.226, f32[2048,768]{1,0:T(8,128)} %get-tuple-element.243, f32[768]{0:T(1024)S(1)} %copy-done.52, bf16[2048,768]{1,0:T(8,128)(2,1)} %all-gather.9.cloned.1.call-done, bf16[768,768]{1,0:T(8,128)(2,1)} %param.22), kind=kOutput, calls=%fused_computation.59 | convolution fusion | flops 2442657024 | bytes 20060160 | tf_op jit(solution)/shard_map/td,fd->tf/dot_general | solution.py:194
  425.4 4.2 convolution_convert_fusion
  431.0 57.7 %reduce-scatter.9.cloned.1.call-done = bf16[512,768]{1,0:T(8,128)(2,1)} async-done(((bf16[2048,768]{1,0:T(8,128)(2,1)}), bf16[512,768]{1,0:T(8,128)(2,1)}) %reduce-scatter.9.cloned.1.call-update) | async-done | bytes 786448 | tf_op jit(solution)/shard_map/reduce_scatter | solution.py:202
  488.7 3.9 multiply_reduce_fusion.1
  497.3 63.6 %all-gather.11.cloned.1.call-done = bf16[2048,768]{1,0:T(8,128)(2,1)} async-done(((bf16[512,768]{1,0:T(8,128)(2,1)}), bf16[2048,768]{1,0:T(8,128)(2,1)}) %all-gather.11.cloned.1.call-update) | async-done | bytes 3145744 | tf_op jit(solution)/shard_map/all_gather | solution.py:212
  560.9 3.1 convolution_convert_fusion.3
  567.5 124.8 %while.27 = (s32[]{:T(128)}, f32[4,512,3,128]{1,0,3,2:T(4,128)}, bf16[4,512,3,64]{1,3,2,0:T(8,128)(2,1)}, bf16[4,512,3,64]{1,3,2,0:T(8,128)(2,1)}, bf16[4,512,3,...) while((s32[]{:T(128)}, f32[4,512,3,128]{1,0,3,2:T(4,128)}, ...), condition=%wide.region_17.18_spmd, body=%wide.region_15.17_spmd.sunk | while | flops 812972544 | bytes 37197472 | solution.py:220
  577.5 16.1 %dynamic_update_slice.31 = f32[4,512,3,128]{1,0,3,2:T(4,128)} dynamic-update-slice(f32[4,512,3,128]{1,0,3,2:T(4,128)} %get-tuple-element.397, f32[1,512,3,128]{1,0,3,2:T(1,128)} %copy.114, s32[]{:T(128)} %get-tuple-element.396, s32[]{:T(128)} %constant.60.clone.1..sunk, s32[]{:T(128)} %constant.60.clone.1..sunk, s32[]{:T(128)} %constant.60.clone.1..sunk) | dynamic-update-slice | bytes 1572868 | tf_op jit(solution)/shard_map/while/body/jit(dynamic_update_index_in_dim)/dynamic_update_slice | solution.py:220
  608.7 16.1 %dynamic_update_slice.31 = f32[4,512,3,128]{1,0,3,2:T(4,128)} dynamic-update-slice(f32[4,512,3,128]{1,0,3,2:T(4,128)} %get-tuple-element.397, f32[1,512,3,128]{1,0,3,2:T(1,128)} %copy.114, s32[]{:T(128)} %get-tuple-element.396, s32[]{:T(128)} %constant.60.clone.1..sunk, s32[]{:T(128)} %constant.60.clone.1..sunk, s32[]{:T(128)} %constant.60.clone.1..sunk) | dynamic-update-slice | bytes 1572868 | tf_op jit(solution)/shard_map/while/body/jit(dynamic_update_index_in_dim)/dynamic_update_slice | solution.py:220
  639.9 16.1 %dynamic_update_slice.31 = f32[4,512,3,128]{1,0,3,2:T(4,128)} dynamic-update-slice(f32[4,512,3,128]{1,0,3,2:T(4,128)} %get-tuple-element.397, f32[1,512,3,128]{1,0,3,2:T(1,128)} %copy.114, s32[]{:T(128)} %get-tuple-element.396, s32[]{:T(128)} %constant.60.clone.1..sunk, s32[]{:T(128)} %constant.60.clone.1..sunk, s32[]{:T(128)} %constant.60.clone.1..sunk) | dynamic-update-slice | bytes 1572868 | tf_op jit(solution)/shard_map/while/body/jit(dynamic_update_index_in_dim)/dynamic_update_slice | solution.py:220
  671.1 16.1 %dynamic_update_slice.31 = f32[4,512,3,128]{1,0,3,2:T(4,128)} dynamic-update-slice(f32[4,512,3,128]{1,0,3,2:T(4,128)} %get-tuple-element.397, f32[1,512,3,128]{1,0,3,2:T(1,128)} %copy.114, s32[]{:T(128)} %get-tuple-element.396, s32[]{:T(128)} %constant.60.clone.1..sunk, s32[]{:T(128)} %constant.60.clone.1..sunk, s32[]{:T(128)} %constant.60.clone.1..sunk) | dynamic-update-slice | bytes 1572868 | tf_op jit(solution)/shard_map/while/body/jit(dynamic_update_index_in_dim)/dynamic_update_slice | solution.py:220
  692.3 3.9 reshape.222
  700.0 2.8 convert_element_type.152
  705.4 2.8 convert_element_type.154
  710.6 4.1 bitcast_convert_fusion
  715.1 7.1 fusion.105
  722.2 4.1 fusion.104
  728.0 3.2 fusion.72
  733.9 44.5 %all-reduce = (f32[2,768]{1,0:T(2,128)}, f32[2,768]{1,0:T(2,128)}, f32[4]{0:T(128)S(1)}) all-reduce(f32[2,768]{1,0:T(2,128)S(1)} %pad_maximum_fusion.8, f32[2,768]{1,0:T(2,128)S(1)} %pad_maximum_fusion.9, f32[4]{0:T(128)S(1)} %pad_maximum_fusion.10), channel_id=1, replica_groups=mesh['dp'=8,'tensor'=4] {'dp','tensor'}, use_global_device_ids=true, to_apply=%region_28.29 | all-reduce | flops 3076 | bytes 24608 | tf_op jit(solution)/shard_map/psum | solution.py:261
  780.6 27.6 %all-reduce.1 = (f32[192,64]{0,1:T(8,128)}, f32[768]{0:T(1024)}) all-reduce(f32[192,64]{0,1:T(8,128)S(1)} %copy.84, f32[768]{0:T(1024)S(1)} %copy-done.44), channel_id=1, replica_groups=mesh['dp'=8,'tensor'=4] {'dp'}, use_global_device_ids=true, to_apply=%region_20.21 | all-reduce | flops 13056 | bytes 104448 | tf_op jit(solution)/shard_map/psum | solution.py:256
  810.4 83.6 %all-reduce.5.cloned.1.call-done = (f32[3,768,192]{1,2,0:T(8,128)}, f32[192,768]{1,0:T(8,128)}, f32[768,768]{1,0:T(8,128)}, f32[768,768]{1,0:T(8,128)}) async-done(((f32[3,768,192]{1,2,0:T(8,128)}, f32[192,768]{1,0:T(8,128)}, f32[768,768]{1,0:T(8,128)}, f32[768,768]{1,0:T(8,128)}), (f32[3,768,192]{1,2,0:T(8,128)}, f32[192,768]{1,0:T(8,128)}, f32[768,768]{1,0:T(8,128)}, ...) | async-done | bytes 7077904 | tf_op jit(solution)/shard_map/psum | solution.py:256
  894.0 2.9 copy.145
  (275 shorter events, 158.8 us)
Async XLA Ops:
  7.2 249.8 %copy-start = (bf16[768,768]{1,0:T(8,128)(2,1)S(1)}, bf16[768,768]{1,0:T(8,128)(2,1)}, u32[]{:S(2)}) copy-start(bf16[768,768]{1,0:T(8,128)(2,1)} %param.20) | copy-start | bytes 3538948
  7.2 68.7 %copy-start.49 = (bf16[3,768,192]{1,2,0:T(8,128)(2,1)S(1)}, bf16[3,768,192]{1,2,0:T(8,128)(2,1)}, u32[]{:S(2)}) copy-start(bf16[3,768,192]{1,2,0:T(8,128)(2,1)} %param.17) | copy-start | bytes 2654212
  7.2 68.6 %all-gather.5.cloned.1.call-start = ((), (), s32[]{:S(2)}) async-start(), calls=%async_computation.4 | async-start | bytes 3932160 | tf_op jit(solution)/shard_map/all_gather | solution.py:132
  7.9 181.0 %reduce-scatter.5.cloned.1.call-start = ((), (), s32[]{:S(2)}) async-start(), calls=%async_computation.5 | async-start | bytes 3932160 | tf_op jit(solution)/shard_map/reduce_scatter | solution.py:154
  79.9 4.8 copy-start.11
  84.7 9.1 %copy-start.17 = (bf16[4,512,3,64]{1,0,3,2:T(4,128)(2,1)S(1)}, bf16[4,512,3,64]{1,0,3,2:T(4,128)(2,1)}, u32[]{:S(2)}) copy-start(bf16[4,512,3,64]{1,0,3,2:T(4,128)(2,1)} %concatenate.27) | copy-start | bytes 2359300
  129.8 59.1 %copy-start.2 = (bf16[512,768]{1,0:T(8,128)(2,1)S(1)}, bf16[512,768]{1,0:T(8,128)(2,1)}, u32[]{:S(2)}) copy-start(bf16[512,768]{1,0:T(8,128)(2,1)} %param.16) | copy-start | bytes 2359300
  129.9 127.1 %all-gather.7.cloned.1.call-start = ((), (), s32[]{:S(2)}) async-start(), calls=%async_computation.6 | async-start | bytes 3932160 | tf_op jit(solution)/shard_map/all_gather | solution.py:163
  131.2 62.2 %copy-start.35 = (f32[768]{0:T(1024)}, f32[768]{0:T(1024)S(1)}, u32[]{:S(2)}) copy-start(f32[768]{0:T(1024)S(1)} %get-tuple-element.170) | copy-start | bytes 9220
  131.2 125.8 %copy-start.51 = (f32[768]{0:T(1024)S(1)}, f32[768]{0:T(1024)}, u32[]{:S(2)}) copy-start(f32[768]{0:T(1024)} %param.21) | copy-start | bytes 9220
  192.0 83.7 %copy-start.36 = (f32[512]{0:T(512)}, f32[512]{0:T(512)S(1)}, u32[]{:S(2)}) copy-start(f32[512]{0:T(512)S(1)} %multiply_reduce_fusion.4) | copy-start | bytes 6148
  193.3 147.1 %reduce-scatter.7.cloned.1.call-start = ((), (), s32[]{:S(2)}) async-start(), calls=%async_computation.7 | async-start | bytes 3932160 | tf_op jit(solution)/shard_map/reduce_scatter | solution.py:169
  257.0 20.4 %copy-start.48 = (bf16[768,768]{1,0:T(8,128)(2,1)S(1)}, bf16[768,768]{1,0:T(8,128)(2,1)}, u32[]{:S(2)}) copy-start(bf16[768,768]{1,0:T(8,128)(2,1)} %param.22) | copy-start | bytes 3538948
  281.3 61.2 %copy-start.15 = (bf16[512,768]{1,0:T(8,128)(2,1)S(1)}, bf16[512,768]{1,0:T(8,128)(2,1)}, u32[]{:S(2)}) copy-start(bf16[512,768]{1,0:T(8,128)(2,1)} %param.27) | copy-start | bytes 2359300
  281.4 131.3 %all-gather.9.cloned.1.call-start = ((), (), s32[]{:S(2)}) async-start(), calls=%async_computation.8 | async-start | bytes 3932160 | tf_op jit(solution)/shard_map/all_gather | solution.py:190
  346.8 65.9 %copy-start.52 = (f32[768]{0:T(1024)S(1)}, f32[768]{0:T(1024)}, u32[]{:S(2)}) copy-start(f32[768]{0:T(1024)} %param.21) | copy-start | bytes 9220
  349.0 139.7 %reduce-scatter.9.cloned.1.call-start = ((), (), s32[]{:S(2)}) async-start(), calls=%async_computation.9 | async-start | bytes 3932160 | tf_op jit(solution)/shard_map/reduce_scatter | solution.py:202
  429.6 59.1 %copy-start.18 = (bf16[512,768]{1,0:T(8,128)(2,1)S(1)}, bf16[512,768]{1,0:T(8,128)(2,1)}, u32[]{:S(2)}) copy-start(bf16[512,768]{1,0:T(8,128)(2,1)} %reduce-scatter.7.cloned.1.call-done) | copy-start | bytes 2359300
  429.6 62.9 %copy-start.37 = (f32[512]{0:T(512)S(1)}, f32[512]{0:T(512)}, u32[]{:S(2)}) copy-start(f32[512]{0:T(512)} %copy-done.36) | copy-start | bytes 6148
  429.7 131.3 %all-gather.11.cloned.1.call-start = ((), (), s32[]{:S(2)}) async-start(), calls=%async_computation.10 | async-start | bytes 3932160 | tf_op jit(solution)/shard_map/all_gather | solution.py:212
  492.6 68.3 %copy-start.34 = (bf16[192,768]{1,0:T(8,128)(2,1)S(1)}, bf16[192,768]{1,0:T(8,128)(2,1)}, u32[]{:S(2)}) copy-start(bf16[192,768]{1,0:T(8,128)(2,1)} %param.19) | copy-start | bytes 884740
  497.3 310.9 %reduce-scatter.11.cloned.1.call-start = ((), (), s32[]{:S(2)}) async-start(), calls=%async_computation.11 | async-start | bytes 3932160 | tf_op jit(solution)/shard_map/reduce_scatter | solution.py:247
  698.5 9.7 %copy-start.24 = (bf16[2048,3,32]{0,2,1:T(8,128)(2,1)S(1)}, bf16[2048,3,32]{0,2,1:T(8,128)(2,1)}, u32[]{:S(2)}) copy-start(bf16[2048,3,32]{0,2,1:T(8,128)(2,1)} %get-tuple-element.234) | copy-start | bytes 1179652
  714.8 7.3 copy-start.47
  714.8 179.2 %all-reduce.5.cloned.1.call-start = ((), (), s32[]{:S(2)}) async-start(), calls=%async_computation.12 | async-start | bytes 14155776 | tf_op jit(solution)/shard_map/psum | solution.py:256
  715.1 7.1 copy-start.55
  722.1 4.2 copy-start.10
  722.2 5.8 copy-start.46
  731.2 48.9 %copy-start.12 = (bf16[1,2048,192]{1,2,0:T(8,128)(2,1)S(1)}, bf16[1,2048,192]{1,2,0:T(8,128)(2,1)}, u32[]{:S(2)}) copy-start(bf16[1,2048,192]{1,2,0:T(8,128)(2,1)} %copy-done.11) | copy-start | bytes 2359300
  731.2 48.9 %copy-start.25 = (bf16[2048,3,32]{0,2,1:T(8,128)(2,1)S(1)}, bf16[2048,3,32]{0,2,1:T(8,128)(2,1)}, u32[]{:S(2)}) copy-start(bf16[2048,3,32]{0,2,1:T(8,128)(2,1)} %get-tuple-element.235) | copy-start | bytes 1179652
  731.2 49.3 %copy-start.44 = (f32[768]{0:T(1024)S(1)}, f32[768]{0:T(1024)}, u32[]{:S(2)}) copy-start(f32[768]{0:T(1024)} %get-tuple-element.217) | copy-start | bytes 9220
  731.2 76.9 %copy-start.8 = (f32[512,768]{1,0:T(8,128)S(1)}, f32[512,768]{1,0:T(8,128)}, u32[]{:S(2)}) copy-start(f32[512,768]{1,0:T(8,128)} %copy-done.7) | copy-start | bytes 4718596
  (36 other events, 72.2 us)
Sparse Core Ops, SparseCore 0:
  9.6 66.1 all-gather.4
  130.0 58.8 reduce-scatter.4
  193.5 63.5 all-gather.6
  281.5 58.8 reduce-scatter.6
  349.1 63.5 all-gather.8
  429.8 58.8 reduce-scatter.8
  497.4 63.5 all-gather.10
  714.9 59.9 reduce-scatter.10
  779.2 114.7 all-reduce.4
where the time goes:
time: 915 us; the launch traced here: 907 us
  waiting for transfers between devices  512 us (56%)
  local copies, waits for them, and re-layouts  132 us (14%)
  matrix products  125 us (14%)
  blocking collectives  72.1 us (8%)
  other arithmetic  50.8 us (6%)
  between operations  15.4 us (2%)
    psum x1, waiting for transfers between devices, per_device(): lax.psum((qkv_grad, rel_grad, out_weight_grad, ffn_in_grad, ffn_bias_grad...  83.6 us
    dynamic_update_slice x8, local copies, waits for them, and re-layouts, per_device(): lax.map(page_backward, paged + (log_totals, to_pages(grad_attended)))  71.2 us
    all_gather x1, waiting for transfers between devices, per_device(): lax.all_gather(grad_two.astype(jnp.bfloat16), 'tensor', axis=0, tiled=True)  63.6 us
    all_gather x1, waiting for transfers between devices, per_device(): whole_attn_grad = lax.all_gather(grad_one_low, 'tensor', axis=0, tiled=True)  63.6 us
    all_gather x1, waiting for transfers between devices, per_device(): lax.all_gather(normed.astype(jnp.bfloat16), 'tensor', axis=0, tiled=True)  63.6 us
    all_gather x1, waiting for transfers between devices, per_device(): whole_tokens = lax.all_gather(tokens, 'tensor', axis=0, tiled=True)  61.9 us
    reduce_scatter x1, waiting for transfers between devices, per_device(): lax.psum_scatter(jnp.dot(lax.slice_in_dim(hidden_low, 0, lax.axis_size('t...  59 us
    reduce_scatter x1, waiting for transfers between devices, per_device(): lax.psum_scatter(jnp.dot(attended_low, out_weight, preferred_element_type...  57.8 us
  transfers between devices with their start and end apart: 9, of which 8 were waited for; matrix products, arithmetic and copies ran while one was open for 3% of the time, Pallas kernels for 0%

commit v1 on v0

v1 whole, which is shorter than its diff:
```python
from functools import partial
import math

import jax
import jax.numpy as jnp
from jax import lax
from jax.experimental import pallas as pl
from jax.experimental.pallas import tpu as pltpu
from jax.sharding import PartitionSpec as P

HEAD_DIM = 64
PAGE = 512
FREQ = 16
POS = 64
SPLIT = 8

norm_epsilon = 1e-05
score_scale = 0.125
masked_score = -1000000000.0

bf16 = jnp.bfloat16
f32 = jnp.float32


def position_features(boxes_rows):
    orders = jnp.arange(FREQ, dtype=jnp.float32)
    rates = 0.5 * jnp.exp(orders * (-math.log(100.0) / FREQ))
    angles = boxes_rows.astype(jnp.float32)[:, None, :] * rates[None, :, None]
    angles = angles.reshape(2 * FREQ, boxes_rows.shape[1])
    return jnp.concatenate([jnp.cos(angles), jnp.sin(angles)], 0).T


def rotate(coeffs, cos_part, sin_part):
    halfway = coeffs.shape[-1] // 2
    first, second = (coeffs[..., :halfway], coeffs[..., halfway:])
    return jnp.concatenate(
        [first * sin_part + second * cos_part, second * sin_part - first * cos_part], -1
    )


def rotate_back(grad_turned, cos_part, sin_part):
    halfway = grad_turned.shape[-1] // 2
    first, second = (grad_turned[..., :halfway], grad_turned[..., halfway:])
    return jnp.concatenate(
        [first * sin_part - second * cos_part, first * cos_part + second * sin_part], -1
    )


def layer_norm(values, gain, shift):
    average = jnp.mean(values, -1, keepdims=True)
    centred = values - average
    spread = jnp.mean(centred * centred, -1, keepdims=True)
    return centred * lax.rsqrt(spread + norm_epsilon) * gain + shift


class Place:
    def __init__(self, dp_size):
        d = lax.axis_index("dp")
        t = lax.axis_index("tensor")
        sub = d % SPLIT
        c = sub % 2
        x = (sub // 2) % 2
        y = sub // 4
        self.d, self.t, self.c = d, t, c
        self.tk = (t, t + 1 - 2 * (t % 2), t + 2 - 4 * (t // 2), 3 - t)
        step_x = (1 - 2 * x) * 2
        step_y = (1 - 2 * y) * 4
        step_1 = (1 - c) * step_x + c * step_y
        step_2 = c * step_x + (1 - c) * step_y
        self.dev_c = d + 1 - 2 * c
        self.dev_1 = d + step_1
        self.dev_2 = d + step_2
        self.yx = sub // 2
        self.yx_1 = (sub + step_1) // 2
        self.yx_2 = (sub + step_2) // 2
        self.yx_12 = (sub + step_1 + step_2) // 2
        self.far = []
        width = SPLIT
        while width < dp_size:
            self.far.append(d + width * (1 - 2 * ((d // width) % 2)))
            width *= 2


def meet(place):
    barrier = pltpu.get_barrier_semaphore()
    targets = [{"dp": v} for v in (place.dev_c, place.dev_1, place.dev_2, *place.far)]
    targets += [{"tensor": place.tk[1]}, {"tensor": place.tk[2]}]
    for target in targets:
        pl.semaphore_signal(barrier, inc=1, device_id=target, device_id_type=pl.DeviceIdType.MESH)
    pl.semaphore_wait(barrier, len(targets))


def remote(source, target, sems, index, device):
    send, recv = sems
    return pltpu.make_async_remote_copy(
        src_ref=source,
        dst_ref=target,
        send_sem=send.at[index],
        recv_sem=recv.at[index],
        device_id=device,
        device_id_type=pl.DeviceIdType.MESH,
    )


def gather_kernel(dp_size, *refs):
    own = refs[0:3]
    rel_own, bias_own = refs[3:5]
    whole = refs[5:8]
    rel_all, bias_all = refs[8:10]
    local_sem, z_send, z_recv, p_send, p_recv, s_send, s_recv = refs[10:]
    zs, ps, ss = (z_send, z_recv), (p_send, p_recv), (s_send, s_recv)
    here = Place(dp_size)
    t, c, yx = here.t, here.c, here.yx
    rows = own[0].shape[2]
    local = []
    for a in range(3):
        local.append(pltpu.make_async_copy(own[a], whole[a].at[t], local_sem.at[a]))
    local.append(pltpu.make_async_copy(rel_own, rel_all.at[t], local_sem.at[3]))
    local.append(pltpu.make_async_copy(bias_own, bias_all.at[t], local_sem.at[4]))
    for copy in local:
        copy.start()
    meet(here)
    t1, t2 = {"tensor": here.tk[1]}, {"tensor": here.tk[2]}
    started = []

    def go(copy):
        copy.start()
        started.append(copy)
        return copy

    small = []
    for i, (mine, every) in enumerate(((rel_own, rel_all), (bias_own, bias_all))):
        small.append(
            (
                go(remote(mine, every.at[t], ss, (i, 0), t1)),
                go(remote(mine, every.at[t], ss, (i, 1), t2)),
            )
        )
    along = []
    for a in range(3):
        piece = own[a].at[yx, c]
        spot = whole[a].at[t, yx, c]
        along.append(
            [go(remote(piece, spot, zs, (a, 0), t1)), go(remote(piece, spot, zs, (a, 1), t2))]
        )
    for i, every in enumerate((rel_all, bias_all)):
        small[i][0].wait_recv()
        spot = every.at[here.tk[1]]
        small[i] = small[i] + (go(remote(spot, spot, ss, (i, 2), t2)),)

    def plane_one(a, k):
        spot = whole[a].at[here.tk[k], yx, c]
        return [go(remote(spot, spot, ps, (a, k, 0), {"dp": here.dev_1}))]

    def plane_two(a, k):
        out = []
        for i, place in enumerate((yx, here.yx_1)):
            spot = whole[a].at[here.tk[k], place, c]
            out.append(go(remote(spot, spot, ps, (a, k, 1 + i), {"dp": here.dev_2})))
        return out

    def plane_three(a, k):
        spot = whole[a].at[here.tk[k], :, c]
        return [go(remote(spot, spot, ps, (a, k, 3), {"dp": here.dev_c}))]

    units = [(a, k) for a in range(3) for k in (1, 2, 3)]
    flight = {}
    for i in range(len(units) + 3):
        if i < len(units):
            a, k = units[i]
            along[a][k - 1].wait_recv()
            if k == 1:
                spot = whole[a].at[here.tk[1], yx, c]
                along[a].append(go(remote(spot, spot, zs, (a, 2), t2)))
            flight[a, k, 1] = plane_one(a, k)
        for lag, step in ((1, plane_two), (2, plane_three)):
            if 0 <= i - lag < len(units):
                a, k = units[i - lag]
                for copy in flight[a, k, lag]:
                    copy.wait_recv()
                flight[a, k, lag + 1] = step(a, k)
        if 0 <= i - 3 < len(units):
            a, k = units[i - 3]
            for copy in flight[a, k, 3]:
                copy.wait_recv()
    for i in range(2):
        small[i][1].wait_recv()
        small[i][2].wait_recv()
    for copy in started:
        copy.wait_send()
    for copy in local:
        copy.wait()


def gather_weights(dp_size, own, rel_own, bias_own):
    vmem = pl.BlockSpec(memory_space=pltpu.VMEM)
    anywhere = pl.BlockSpec(memory_space=pl.ANY)
    shapes = [jax.ShapeDtypeStruct((4,) + a.shape, a.dtype) for a in (*own, rel_own, bias_own)]
    dma = pltpu.SemaphoreType.DMA
    return pl.pallas_call(
        partial(gather_kernel, dp_size),
        out_shape=shapes,
        in_specs=[anywhere] * 5,
        out_specs=[vmem] * 5,
        scratch_shapes=[
            dma((5,)),
            dma((3, 3)),
            dma((3, 3)),
            dma((3, 4, 4)),
            dma((3, 4, 4)),
            dma((2, 3)),
            dma((2, 3)),
        ],
        compiler_params=pltpu.CompilerParams(
            collective_id=0, has_side_effects=True, vmem_limit_bytes=60 * 1024 * 1024
        ),
        name="gather_weights",
    )(*own, rel_own, bias_own)


def reduce_kernel(dp_size, n_far, *refs):
    grads_in = refs[0:4]
    sums_in = refs[4]
    outs = refs[5:9]
    sums_out = refs[9]
    grads = refs[10:14]
    got_c = refs[14:18]
    got_1 = refs[18:22]
    got_2 = refs[22:26]
    got_z = refs[26:30]
    got_far = refs[30:34]
    sums_tx, sums_rx = refs[34:36]
    local_sem, g_send, g_recv, f_send, f_recv, s_send, s_recv = refs[36:]
    gs, fs, sm = (g_send, g_recv), (f_send, f_recv), (s_send, s_recv)
    here = Place(dp_size)
    c, yx = here.c, here.yx
    arrays = range(4)
    local = {}
    for a in arrays:
        for k in (3, 2, 1, 0):
            copy = pltpu.make_async_copy(
                grads_in[a].at[here.tk[k]], grads[a].at[here.tk[k]], local_sem.at[a, k]
            )
            copy.start()
            local[a, k] = copy
    meet(here)
    started = []

    def go(copy):
        copy.start()
        started.append(copy)
        return copy

    t1, t2 = {"tensor": here.tk[1]}, {"tensor": here.tk[2]}
    butterfly = [{"dp": here.dev_c}, {"dp": here.dev_1}, {"dp": here.dev_2}, t1, t2]
    butterfly += [{"dp": v} for v in here.far]
    sums_tx[0] = sums_in[...]
    flow = {}
    sums_flow = [go(remote(sums_tx.at[0], sums_rx.at[0], sm, (0,), butterfly[0]))]

    def sums_step(i):
        sums_flow[i].wait_recv()
        total = sums_tx[i] + sums_rx[i]
        if i + 1 < len(butterfly):
            sums_tx[i + 1] = total
            sums_flow.append(
                go(remote(sums_tx.at[i + 1], sums_rx.at[i + 1], sm, (i + 1,), butterfly[i + 1]))
            )
        else:
            sums_out[...] = total

    def start_c(a, k):
        local[a, k].wait()
        tk = here.tk[k]
        flow[a, k, 0] = [
            go(
                remote(
                    grads[a].at[tk, :, 1 - c], got_c[a].at[k], gs, (a, k, 0), {"dp": here.dev_c}
                )
            )
        ]

    def take_c(a, k):
        tk = here.tk[k]
        flow[a, k, 0][0].wait_recv()

        def body(i, carry):
            grads[a][tk, i, c] = grads[a][tk, i, c] + got_c[a][k, i]
            return carry

        lax.fori_loop(0, 4, body, 0)
        flow[a, k, 1] = [
            go(
                remote(
                    grads[a].at[tk, here.yx_1, c],
                    got_1[a].at[k, 0],
                    gs,
                    (a, k, 1),
                    {"dp": here.dev_1},
                )
            ),
            go(
                remote(
                    grads[a].at[tk, here.yx_12, c],
                    got_1[a].at[k, 1],
                    gs,
                    (a, k, 2),
                    {"dp": here.dev_1},
                )
            ),
        ]

    def take_1(a, k):
        tk = here.tk[k]
        for copy in flow[a, k, 1]:
            copy.wait_recv()
        grads[a][tk, here.yx_2, c] = grads[a][tk, here.yx_2, c] + got_1[a][k, 1]
        flow[a, k, 2] = [
            go(
                remote(
                    grads[a].at[tk, here.yx_2, c],
                    got_2[a].at[k],
                    gs,
                    (a, k, 3),
                    {"dp": here.dev_2},
                )
            )
        ]
        grads[a][tk, yx, c] = grads[a][tk, yx, c] + got_1[a][k, 0]

    def take_2(a, k):
        tk = here.tk[k]
        flow[a, k, 2][0].wait_recv()
        grads[a][tk, yx, c] = grads[a][tk, yx, c] + got_2[a][k]
        if k >= 2:
            flow[a, k, 3] = [
                go(remote(grads[a].at[tk, yx, c], got_z[a].at[k - 2], gs, (a, k, 4), t2))
            ]
        else:
            flow[a, k + 2, 3][0].wait_recv()
            grads[a][tk, yx, c] = grads[a][tk, yx, c] + got_z[a][k]
            if k == 1:
                flow[a, 1, 3] = [
                    go(remote(grads[a].at[tk, yx, c], got_z[a].at[2], gs, (a, 1, 4), t1))
                ]

    def take_z(a):
        tk = here.tk[0]
        flow[a, 1, 3][0].wait_recv()
        grads[a][tk, yx, c] = grads[a][tk, yx, c] + got_z[a][2]
        for i, v in enumerate(here.far):
            copy = go(remote(grads[a].at[tk, yx, c], got_far[a].at[i], fs, (a, 4 + i), {"dp": v}))
            copy.wait()
            grads[a][tk, yx, c] = grads[a][tk, yx, c] + got_far[a][i]
        outs[a][yx, c] = grads[a][tk, yx, c]
        spot = outs[a].at[yx, c]
        flow[a, 0] = [go(remote(spot, spot, fs, (a, 0), {"dp": here.dev_1}))]

    def back_1(a):
        flow[a, 0][0].wait_recv()
        flow[a, 1] = []
        for i, place in enumerate((yx, here.yx_1)):
            spot = outs[a].at[place, c]
            flow[a, 1].append(go(remote(spot, spot, fs, (a, 1 + i), {"dp": here.dev_2})))

    def back_2(a):
        for copy in flow[a, 1]:
            copy.wait_recv()
        spot = outs[a].at[:, c]
        flow[a, 2] = [go(remote(spot, spot, fs, (a, 3), {"dp": here.dev_c}))]

    def back_3(a):
        flow[a, 2][0].wait_recv()

    units = [(a, k) for a in arrays for k in (3, 2, 1, 0)]
    for a, k in units:
        start_c(a, k)
    for i in range(len(units) + 8):
        if i < len(units):
            take_c(*units[i])
        if 0 <= i - 1 < len(units):
            take_1(*units[i - 1])
        if i < len(butterfly):
            sums_step(i)
        if 0 <= i - 2 < len(units):
            take_2(*units[i - 2])
        for lag, step in ((3, take_z), (4, back_1), (5, back_2), (6, back_3)):
            j = i - lag
            if 0 <= j < len(units) and units[j][1] == 0:
                step(units[j][0])
    for i in range(len(units) + 8, len(butterfly)):
        sums_step(i)
    for copy in started:
        copy.wait_send()


def reduce_grads(dp_size, grads, sums):
    vmem = pl.BlockSpec(memory_space=pltpu.VMEM)
    anywhere = pl.BlockSpec(memory_space=pl.ANY)
    n_far = max(0, (dp_size // SPLIT).bit_length() - 1)
    steps = 5 + n_far
    dma = pltpu.SemaphoreType.DMA
    scratch = []
    pieces = [g.shape[3:] for g in grads]
    types = [g.dtype for g in grads]
    for lead in ((4, 4, 2), (4, 4), (4, 2), (4,), (3,), (max(1, n_far),)):
        scratch += [pltpu.VMEM(lead + p, k) for p, k in zip(pieces, types)]
    scratch += [pltpu.VMEM((steps,) + sums.shape, f32)] * 2
    scratch += [
        dma((4, 4)),
        dma((4, 4, 5)),
        dma((4, 4, 5)),
        dma((4, 4 + max(1, n_far))),
        dma((4, 4 + max(1, n_far))),
        dma((steps,)),
        dma((steps,)),
    ]
    shapes = [jax.ShapeDtypeStruct((4, 2) + p, k) for p, k in zip(pieces, types)]
    shapes.append(jax.ShapeDtypeStruct(sums.shape, f32))
    return pl.pallas_call(
        partial(reduce_kernel, dp_size, n_far),
        out_shape=shapes,
        in_specs=[anywhere] * 4 + [vmem],
        out_specs=[vmem] * 5,
        scratch_shapes=scratch,
        compiler_params=pltpu.CompilerParams(
            collective_id=1, has_side_effects=True, vmem_limit_bytes=60 * 1024 * 1024
        ),
        name="reduce_grads",
    )(*grads, sums)


def per_device(
    dp_size,
    tokens,
    qkv_weight,
    rel_weight,
    out_weight,
    ffn_in_weight,
    ffn_in_bias,
    ffn_out_weight,
    norm_gains,
    norm_biases,
    page_lengths,
    boxes,
    out_grad,
):
    rows, width = tokens.shape
    part = out_weight.shape[0]
    shards = boxes.shape[1] // rows
    heads_part = part // HEAD_DIM
    heads = heads_part * shards
    t = lax.axis_index("tensor")
    boxes_page = lax.dynamic_slice(boxes, (0, t * rows), (2, rows))
    length = lax.dynamic_index_in_dim(page_lengths, t, 0, keepdims=False)
    features = position_features(boxes_page)
    halfway = POS // 2
    cos_part = features[:, None, :halfway]
    sin_part = features[:, None, halfway:]
    key_valid = jnp.arange(rows, dtype=jnp.int32) < length
    valid_rows = key_valid.astype(f32)[:, None]

    attn_own = jnp.concatenate(
        [jnp.transpose(qkv_weight, (0, 2, 1)).reshape(3 * part, width), out_weight], 0
    )
    split = lambda w: w.reshape(4, 2, w.shape[0] // SPLIT, w.shape[1])
    rel_own = jnp.pad(rel_weight, ((0, 0), (0, 128 - POS)))
    attn_all, in_all, out_all, rel_all, bias_all = gather_weights(
        dp_size,
        (split(attn_own), split(ffn_in_weight), split(ffn_out_weight)),
        rel_own,
        ffn_in_bias.reshape(1, -1),
    )
    attn_all = attn_all.reshape(shards, 4 * part, width)
    qkv_all = attn_all[:, : 3 * part].reshape(shards, 3, part, width)
    proj_out = attn_all[:, 3 * part :].reshape(shards * part, width)
    w_in = in_all.reshape(shards, width, -1)
    w_out = out_all.reshape(-1, width)
    relation = rel_all[:, :, :POS].reshape(heads, HEAD_DIM, POS)
    bias = bias_all.reshape(shards, -1)

    projected = jnp.einsum("td,scnd->ctsn", tokens, qkv_all, preferred_element_type=f32).astype(
        bf16
    )
    projected = projected.reshape(3, rows, heads, HEAD_DIM)
    queries, keys_head, values = projected[0], projected[1], projected[2]
    coeffs = jnp.einsum("thd,hdp->thp", queries, relation, preferred_element_type=f32)
    turned = rotate(coeffs, cos_part, sin_part).astype(bf16)
    placed = jnp.broadcast_to(features.astype(bf16)[:, None, :], (rows, heads, POS))
    query_full = jnp.concatenate([queries, turned], -1)
    key_full = jnp.concatenate([keys_head, placed], -1)
    scores = (
        jnp.einsum("qhe,khe->hqk", query_full, key_full, preferred_element_type=f32) * score_scale
    )
    scores = jnp.where(key_valid[None, None, :], scores, masked_score)
    raised = jnp.exp(scores - jnp.max(scores, -1, keepdims=True))
    probs = raised / jnp.sum(raised, -1, keepdims=True)
    weights = probs.astype(bf16)
    attended = (
        jnp.einsum("hqk,khd->qhd", weights, values, preferred_element_type=f32)
        .astype(bf16)
        .reshape(rows, heads * HEAD_DIM)
    )
    attn_out = jnp.dot(attended, proj_out, preferred_element_type=f32)
    tokens_value = tokens.astype(f32)
    normed, norm_back_one = jax.vjp(
        layer_norm, tokens_value + attn_out, norm_gains[0], norm_biases[0]
    )
    normed_low = normed.astype(bf16)
    hidden_pre = (
        jnp.einsum("td,sdf->tsf", normed_low, w_in, preferred_element_type=f32) + bias[None]
    ).reshape(rows, -1)
    hidden_act, gelu_back = jax.vjp(partial(jax.nn.gelu, approximate=False), hidden_pre)
    hidden_low = hidden_act.astype(bf16)
    ffn_out = jnp.dot(hidden_low, w_out, preferred_element_type=f32)
    result, norm_back_two = jax.vjp(layer_norm, normed + ffn_out, norm_gains[1], norm_biases[1])
    stats = jnp.stack(
        [
            jnp.sum(valid_rows * tokens_value * tokens_value),
            jnp.sum(valid_rows * attn_out * attn_out),
            jnp.sum(valid_rows * ffn_out * ffn_out),
            jnp.sum(valid_rows) * width,
        ]
    )
    grad_two, gain_two, shift_two = norm_back_two(out_grad.astype(f32))
    grad_ffn = grad_two.astype(bf16)
    ffn_out_grad = jnp.einsum("tf,td->fd", hidden_low, grad_ffn, preferred_element_type=f32)
    grad_hidden = jnp.einsum("td,fd->tf", grad_ffn, w_out, preferred_element_type=f32)
    grad_pre = gelu_back(grad_hidden)[0].astype(bf16)
    ffn_bias_grad = jnp.sum(grad_pre.astype(f32), 0)
    grad_pre_parts = grad_pre.reshape(rows, shards, -1)
    ffn_in_grad = jnp.einsum("td,tsf->sdf", normed_low, grad_pre_parts, preferred_element_type=f32)
    grad_normed = grad_two + jnp.einsum(
        "tsf,sdf->td", grad_pre_parts, w_in, preferred_element_type=f32
    )
    grad_one, gain_one, shift_one = norm_back_one(grad_normed)
    grad_one_low = grad_one.astype(bf16)
    out_weight_grad = jnp.einsum("th,td->hd", attended, grad_one_low, preferred_element_type=f32)
    grad_attended = (
        jnp.einsum("td,hd->th", grad_one_low, proj_out, preferred_element_type=f32)
        .astype(bf16)
        .reshape(rows, heads, HEAD_DIM)
    )
    grad_weights = jnp.einsum("qhd,khd->hqk", grad_attended, values, preferred_element_type=f32)
    inner = jnp.sum(probs * grad_weights, -1, keepdims=True)
    grad_scores = (probs * (grad_weights - inner)).astype(bf16)
    grad_query_full = (
        jnp.einsum("hqk,khe->qhe", grad_scores, key_full, preferred_element_type=f32) * score_scale
    )
    grad_keys = (
        jnp.einsum("hqk,qhe->khe", grad_scores, queries, preferred_element_type=f32) * score_scale
    ).astype(bf16)
    grad_values = jnp.einsum(
        "hqk,qhd->khd", weights, grad_attended, preferred_element_type=f32
    ).astype(bf16)
    grad_turned = grad_query_full[..., HEAD_DIM:].astype(bf16)
    grad_coeffs = rotate_back(grad_turned.astype(f32), cos_part, sin_part).astype(bf16)
    grad_queries = (
        grad_query_full[..., :HEAD_DIM]
        + jnp.einsum("thp,hdp->thd", grad_coeffs, relation, preferred_element_type=f32)
    ).astype(bf16)
    rel_grad = jnp.einsum("thd,thp->hdp", queries, grad_coeffs, preferred_element_type=f32)
    grad_projected = jnp.stack([grad_queries, grad_keys, grad_values]).reshape(
        3, rows, shards, part
    )
    qkv_grad = jnp.einsum("td,ctsn->scnd", tokens, grad_projected, preferred_element_type=f32)
    tokens_grad = (
        grad_one
        + jnp.einsum("ctsn,scnd->td", grad_projected, qkv_all, preferred_element_type=f32)
    ).astype(bf16)

    attn_grad = jnp.concatenate(
        [
            qkv_grad.reshape(shards, 3 * part, width),
            out_weight_grad.reshape(shards, part, width),
        ],
        1,
    ).astype(bf16)
    split4 = lambda g: g.reshape(shards, 4, 2, g.shape[1] // SPLIT, g.shape[2])
    rel_parts = rel_grad.reshape(shards, heads_part, HEAD_DIM, POS)
    rel_parts = jnp.transpose(rel_parts, (0, 2, 1, 3)).reshape(shards, HEAD_DIM, heads_part * POS)
    rel_parts = jnp.pad(rel_parts, ((0, 0), (0, 0), (0, 256 - heads_part * POS)))
    sums = jnp.concatenate(
        [
            jnp.stack([gain_one, gain_two, shift_one, shift_two]),
            ffn_bias_grad.reshape(shards, -1),
            jnp.pad(stats[None], ((0, 0), (0, width - 4))),
            jnp.zeros((16 - 5 - shards, width), f32),
        ],
        0,
    )
    attn_sum, in_sum, out_sum, rel_sum, sums = reduce_grads(
        dp_size,
        (
            split4(attn_grad),
            split4(ffn_in_grad.astype(bf16)),
            split4(ffn_out_grad.astype(bf16).reshape(shards, -1, width)),
            split4(rel_parts),
        ),
        sums,
    )
    attn_sum = attn_sum.reshape(4 * part, width)
    qkv_sum = jnp.transpose(attn_sum[: 3 * part].reshape(3, part, width), (0, 2, 1)).astype(f32)
    rel_out = jnp.transpose(
        rel_sum.reshape(HEAD_DIM, 256)[:, : heads_part * POS].reshape(HEAD_DIM, heads_part, POS),
        (1, 0, 2),
    ).reshape(part, POS)
    bias_out = lax.dynamic_index_in_dim(sums, 4 + t, 0, keepdims=False)
    stats_total = sums[4 + shards]
    return (
        result.astype(bf16),
        tokens_grad,
        qkv_sum,
        rel_out,
        attn_sum[3 * part :].astype(f32),
        in_sum.reshape(width, -1).astype(f32),
        bias_out,
        out_sum.reshape(-1, width).astype(f32),
        sums[0:2],
        sums[2:4],
        jnp.sqrt(stats_total[:3] / stats_total[3]),
    )


def solution(mesh):
    return jax.shard_map(
        partial(per_device, mesh.shape["dp"]),
        mesh=mesh,
        in_specs=(
            P(("dp", "tensor"), None),
            P(None, None, "tensor"),
            P("tensor", None),
            P("tensor", None),
            P(None, "tensor"),
            P("tensor"),
            P("tensor", None),
            P(),
            P(),
            P("dp"),
            P(None, "dp"),
            P(("dp", "tensor"), None),
        ),
        out_specs=(
            P(("dp", "tensor"), None),
            P(("dp", "tensor"), None),
            P(None, None, "tensor"),
            P("tensor", None),
            P("tensor", None),
            P(None, "tensor"),
            P("tensor"),
            P("tensor", None),
            P(),
            P(),
            P(),
        ),
        check_vma=False,
    )
```

time: 915 us -> 413 us (0.45)
  waiting for transfers between devices: 512 us -> 0 us
  Pallas kernels: 0 us -> 184 us
  blocking collectives: 72.1 us -> 0 us
  local copies, waits for them, and re-layouts: 132 us -> 61.2 us
  matrix products: 125 us -> 107 us
  between operations: 15.4 us -> 2.28 us
    all_gather x4 -> x0, waiting for transfers between devices: 253 us -> none  [the longest x1 63.6 us: per_device(): lax.all_gather(grad_two.astype(jnp.bfloat16), 'tensor', axis=0, tiled=True)]
    pallas_call x0 -> x2, Pallas kernels: none -> 184 us  [the longest x1 101 us: reduce_grads(): pl.pallas_call(partial(reduce_kernel, dp_size, n_far), out_shape=shapes,...]
    reduce_scatter x4 -> x0, waiting for transfers between devices: 174 us -> none  [the longest x1 59 us: per_device(): lax.psum_scatter(jnp.dot(lax.slice_in_dim(hidden_low, 0, lax.axis_size('t...]
    psum x1 -> x0, waiting for transfers between devices: 83.6 us -> none  [per_device(): lax.psum((qkv_grad, rel_grad, out_weight_grad, ffn_in_grad, ffn_bias_grad...]
    dynamic_update_slice x12 -> x0, local copies, waits for them, and re-layouts: 74 us -> none  [the longest x8 71.2 us: per_device(): lax.map(page_backward, paged + (log_totals, to_pages(grad_attended)))]
    psum x2 -> x0, blocking collectives: 72.1 us -> none  [the longest x1 44.5 us: per_device(): lax.psum((gains_local, shifts_local), ('dp', 'tensor'))]
    mul x0 -> x4, local copies, waits for them, and re-layouts: none -> 27 us  [per_device(): jax.vjp(partial(jax.nn.gelu, approximate=False), hidden_pre)]
    dot_general x42 -> x20, matrix products: 123 us -> 106 us  [the longest x1 19.5 us: per_device(): jnp.einsum('td,sdf->tsf', normed_low, w_in, preferred_element_type=f32)]
  transfers between devices with their start and end apart: 9 -> 0, of which waited for: 8 -> 0; matrix products, arithmetic and copies ran while one was open for 3% -> 0% of each run, Pallas kernels for 0% -> 0%
where the time goes in v1:
time: 413 us; the launch traced here: 408 us
  Pallas kernels  184 us (45%)
  matrix products  107 us (26%)
  local copies, waits for them, and re-layouts  61.2 us (15%)
  other arithmetic  54 us (13%)
    pallas_call x1, Pallas kernels, reduce_grads(): pl.pallas_call(partial(reduce_kernel, dp_size, n_far), out_shape=shapes,...  101 us
    pallas_call x1, Pallas kernels, gather_weights(): pl.pallas_call(partial(gather_kernel, dp_size), out_shape=shapes, in_spec...  82.8 us
    mul x4, local copies, waits for them, and re-layouts, per_device(): jax.vjp(partial(jax.nn.gelu, approximate=False), hidden_pre)  27 us
    dot_general x1, matrix products, per_device(): jnp.einsum('td,sdf->tsf', normed_low, w_in, preferred_element_type=f32)  19.5 us
    another operation x1, other arithmetic, per_device(): jax.vjp(partial(jax.nn.gelu, approximate=False), hidden_pre)  14.7 us
    dot_general x1, matrix products, per_device(): jnp.einsum('td,fd->tf', grad_ffn, w_out, preferred_element_type=f32)  13.9 us
    dot_general x1, matrix products, per_device(): jnp.einsum('qhd,khd->hqk', grad_attended, values, preferred_element_type=...  10.4 us
    sub x1, other arithmetic, per_device(): raised = jnp.exp(scores - jnp.max(scores, -1, keepdims=True))  8.96 us

profile of v1, /device:TPU:0, one launch (start us, length us, event | category | flops | bytes accessed | tf_op | source)
XLA Modules:
  0.0 408.3 jit_solution(13266043978862418736)
XLA Ops:
  9.3 2.4 pad_maximum_fusion.3
  12.0 82.8 %gather_weights.1 = (bf16[4,4,2,96,768]{4,3,2,1,0:T(8,128)(2,1)}, bf16[4,4,2,96,768]{4,3,2,1,0:T(8,128)(2,1)}, bf16[4,4,2,96,768]{4,3,2,1,0:T(8,128)(2,1)}, bf16[4,192,128]{2,1,0:T(8,128)(2,1)}, f32[4,1,768]{2,1,0:T(1,128)}) custom-call(bf16[4,2,96,768]{3,2,1,0:T(8,128)(2,1)} %bitcast.173, bf16[4,2,96,768]{3,2,1,0:T(8,128)(2,1)} %bitcast.181, ...), custom_call_target="tpu_custom_call" | custom-call | tf_op jit(solution)/shard_map/gather_weights/pallas_call | solution.py:200
  95.5 2.4 slice.119
  98.0 2.2 slice.111
  100.2 2.1 convert_bitcast_fusion.1
  105.8 2.1 convolution_bitcast_fusion
  110.1 9.0 %fusion.94 = (f32[12,512]{1,0:T(8,128)S(1)}, f32[12,512,512]{1,2,0:T(8,128)}) fusion(f32[12,512,512]{1,2,0:T(8,128)S(1)} %fusion.43, pred[512]{0:T(512)(128)(4,1)S(1)} %get-tuple-element.90), kind=kOutput, calls=%fused_computation.171 | output fusion | flops 18874880 | bytes 25190912 | tf_op jit(solution)/shard_map/sub | solution.py:496
  119.1 6.0 %fusion.54 = bf16[12,64,512]{2,1,0:T(8,128)(2,1)S(1)} fusion(bf16[512,12,64]{0,2,1:T(8,128)(2,1)S(1)} %bitcast.185, f32[12,512,512]{1,2,0:T(8,128)} %get-tuple-element.83, f32[12,512]{1,0:T(8,128)S(1)} %get-tuple-element.82), kind=kOutput, calls=%fused_computation.107 | convolution fusion | flops 409337856 | bytes 14180352 | tf_op jit(solution)/shard_map/hqk,khd->qhd/dot_general | solution.py:500
  127.5 19.5 %fusion.4 = (bf16[512,4,768]{2,0,1:T(8,128)(2,1)}, f32[512,4,768]{2,0,1:T(8,128)}, f32[512,4,768]{2,0,1:T(8,128)}) fusion(f32[4,768]{1,0:T(4,128)S(1)} %bitcast.201, bf16[4,768,768]{2,1,0:T(8,128)(2,1)S(1)} %bitcast.205, f32[512,768]{1,0:T(8,128)S(1)} %get-tuple-element.65, f32[768]{0:T(1024)S(1)} %get-tuple-element.51, f32[768]{0:T(1024)S(1)} %get-tuple-element.92, ...), kind=kOutput, calls=%fused_computation.10 | convolution fusion | flops 2521694208 | bytes 22042624 | tf_op jit(solution)/shard_map/td,sdf->tsf/dot_general | solution.py:511
  146.9 4.9 %copy.47 = bf16[512,4,768]{0,2,1:T(8,128)(2,1)} copy(bf16[512,4,768]{2,0,1:T(8,128)(2,1)} %get-tuple-element.61) | data formatting | bytes 6291456 | tf_op jit(solution)/shard_map/convert_element_type | solution.py:514
  151.8 7.8 %fusion.39 = (f32[]{:T(128)}, f32[]{:T(128)}, f32[]{:T(128)}, f32[512]{0:T(512)S(1)}, f32[512,768]{1,0:T(8,128)S(1)}) fusion(bf16[512,768]{1,0:T(8,128)(2,1)} %param.12, f32[512]{0:T(512)S(1)} %get-tuple-element.91, f32[512,768]{1,0:T(8,128)} %get-tuple-element.84, f32[768]{0:T(1024)S(1)} %get-tuple-element.51, f32[768]{0:T(1024)S(1)} %get-tuple-element.92, ...), kind=kOutput, calls=%fused_computation.79 | convolution fusion | flops 2422210048 | bytes 13383692 | tf_op jit(solution)/shard_map/dot_general | solution.py:515
  159.6 2.0 maximum_bitcast_fusion.1
  162.7 2.1 fusion.87
  164.8 6.6 %copy.50 = f32[512,4,768]{0,2,1:T(8,128)} copy(f32[512,4,768]{2,0,1:T(8,128)} %get-tuple-element.62) | data formatting | bytes 12582912 | tf_op jit(solution)/shard_map/jvp()/mul | solution.py:513
  171.4 6.6 %copy.51 = f32[512,3072]{1,0:T(8,128)} copy(f32[512,3072]{0,1:T(8,128)} %bitcast.161) | data formatting | bytes 12582912 | tf_op jit(solution)/shard_map/jvp()/mul | solution.py:513
  178.0 14.7 %fusion.5 = f32[512,3072]{1,0:T(8,128)} fusion(f32[512,3072]{1,0:T(8,128)} %copy.51), kind=kLoop, calls=%fused_computation.11 | loop fusion | flops 94371840 | bytes 12582912 | tf_op jit(solution)/shard_map/jvp()/erfc | solution.py:513
  192.7 6.6 %copy.48 = f32[512,4,768]{0,2,1:T(8,128)} copy(f32[512,4,768]{2,0,1:T(8,128)} %get-tuple-element.63) | data formatting | bytes 12582912 | tf_op jit(solution)/shard_map/jvp()/mul | solution.py:513
  199.4 7.2 %copy.49 = f32[512,3072]{1,0:T(8,128)} copy(f32[512,3072]{0,1:T(8,128)} %bitcast.162) | data formatting | bytes 12582912 | tf_op jit(solution)/shard_map/jvp()/mul | solution.py:513
  206.6 13.9 %convert_reduce_fusion = (f32[3072]{0:T(1024)S(1)}, bf16[512,3072]{1,0:T(8,128)(2,1)}) fusion(f32[512,3072]{1,0:T(8,128)} %fusion.5, f32[512,3072]{1,0:T(8,128)} %copy.51, f32[512,3072]{1,0:T(8,128)} %copy.49, bf16[3072,768]{1,0:T(8,128)(2,1)} %bitcast.207, f32[512,768]{1,0:T(8,128)} %get-tuple-element.58, f32[512]{0:T(512)S(1)} %negate_multiply_fusion.2), kind=kOutput, calls=%fused_computation.12 | convolution fusion | flops 2437149696 | bytes 28325888 | tf_op jit(solution)/shard_map/td,fd->tf/dot_general | solution.py:528
  220.5 8.5 %convolution_convert_fusion = bf16[3072,768]{1,0:T(8,128)(2,1)} fusion(f32[512,3072]{1,0:T(8,128)} %copy.49, f32[512,3072]{1,0:T(8,128)S(1)} %bitcast.159, f32[512,768]{1,0:T(8,128)S(1)} %copy-done.9, f32[512]{0:T(512)S(1)} %negate_multiply_fusion.2), kind=kOutput, calls=%fused_computation.46 | convolution fusion | flops 2422210560 | bytes 18876416 | tf_op jit(solution)/shard_map/tf,td->fd/dot_general | solution.py:527
  229.0 6.6 %multiply_reduce_fusion.1 = (f32[768]{0:T(1024)S(1)}, f32[512]{0:T(512)S(1)}, f32[768]{0:T(1024)S(1)}, f32[512,768]{1,0:T(8,128)}) fusion(f32[512,768]{1,0:T(8,128)S(1)} %copy-done.5, f32[512]{0:T(512)S(1)} %fusion.70, f32[512]{0:T(512)S(1)} %broadcast_multiply_fusion.1, f32[768]{0:T(1024)S(1)} %get-tuple-element.92, bf16[4,768,768]{2,1,0:T(8,128)(2,1)} %bitcast.202, ...), kind=kOutput, calls=%fused_computation.95 | convolution fusion | flops 2419849216 | bytes 12600320 | tf_op jit(solution)/shard_map/tsf,sdf->td/dot_general | solution.py:533
  235.7 2.1 fusion.86
  238.1 4.9 %fusion.30 = bf16[4,768,768]{1,2,0:T(8,128)(2,1)} fusion(bf16[64,4,8,768]{3,2,1,0:T(8,128)(2,1)S(1)} %bitcast.209, f32[512,768]{1,0:T(8,128)S(1)} %copy-done.6, f32[768]{0:T(1024)S(1)} %get-tuple-element.51, f32[768]{0:T(1024)S(1)} %get-tuple-element.92, f32[512]{0:T(512)S(1)} %fusion.70, f32[512]{0:T(512)S(1)} %broadcast_multiply_fusion.1), kind=kOutput, calls=%fused_computation.60 | convolution fusion | flops 2420244480 | bytes 9447424 | tf_op jit(solution)/shard_map/td,tsf->sdf/dot_general | solution.py:532
  245.4 2.5 convolution_convert_fusion.1
  247.9 6.7 %fusion.57 = bf16[12,64,512]{2,1,0:T(8,128)(2,1)S(1)} fusion(bf16[512,12,64]{0,2,1:T(8,128)(2,1)S(1)} %bitcast.189, f32[12,512,512]{1,2,0:T(8,128)} %get-tuple-element.83, f32[12,512]{1,0:T(8,128)S(1)} %get-tuple-element.82), kind=kOutput, calls=%fused_computation.108 | convolution fusion | flops 409337856 | bytes 14180352 | tf_op jit(solution)/shard_map/hqk,qhd->khd/dot_general | solution.py:553
  254.7 10.4 %multiply_reduce_fusion = (f32[12,512]{1,0:T(8,128)S(1)}, f32[12,512,512]{1,2,0:T(8,128)}) fusion(f32[12,512,512]{1,2,0:T(8,128)} %get-tuple-element.83, f32[12,512]{1,0:T(8,128)S(1)} %get-tuple-element.82, bf16[512,12,64]{0,2,1:T(8,128)(2,1)S(1)} %bitcast.190, bf16[512,12,64]{0,2,1:T(8,128)(2,1)S(1)} %bitcast.186), kind=kOutput, calls=%fused_computation.2 | convolution fusion | flops 412084224 | bytes 26787840 | tf_op jit(solution)/shard_map/qhd,khd->hqk/dot_general | solution.py:544
  267.5 7.0 %multiply_convert_fusion = bf16[12,512,512]{1,2,0:T(8,128)(2,1)S(1)} fusion(f32[12,512,512]{1,2,0:T(8,128)} %get-tuple-element.87, f32[12,512]{1,0:T(8,128)S(1)} %get-tuple-element.86, f32[12,512,512]{1,2,0:T(8,128)S(1)} %bitcast.170, f32[12,512]{1,0:T(8,128)S(1)} %get-tuple-element.82), kind=kLoop, calls=%fused_computation.1 | loop fusion | flops 12582912 | bytes 31506432 | tf_op jit(solution)/shard_map/convert_element_type | solution.py:546
  276.4 2.0 multiply_convert_fusion.3
  281.2 3.0 fusion.49
  285.0 3.4 convert_bitcast_fusion
  288.7 2.4 pad_maximum_fusion
  291.1 101.4 %reduce_grads.1 = (bf16[4,2,96,768]{3,2,1,0:T(8,128)(2,1)}, bf16[4,2,96,768]{3,2,1,0:T(8,128)(2,1)}, bf16[4,2,96,768]{3,2,1,0:T(8,128)(2,1)}, f32[4,2,8,256]{3,2,1,0:T(8,128)}, f32[16,768]{1,0:T(8,128)}) custom-call(bf16[4,4,2,96,768]{4,3,2,1,0:T(8,128)(2,1)} %bitcast.163, bf16[4,4,2,96,768]{4,3,2,1,0:T(8,128)(2,1)} %bitcast.176, ...), custom_call_target="tpu_custom_call" | custom-call | tf_op jit(solution)/shard_map/reduce_grads/pallas_call | solution.py:420
  (150 shorter events, 44.2 us)
Async XLA Ops:
  9.2 98.8 %copy-start.27 = (f32[512,32]{0,1:T(8,128)}, f32[512,32]{0,1:T(8,128)S(1)}, u32[]{:S(2)}) copy-start(f32[512,32]{0,1:T(8,128)S(1)} %get-tuple-element.76) | copy-start | bytes 196612
  9.2 98.8 %copy-start.29 = (f32[512,32]{0,1:T(8,128)}, f32[512,32]{0,1:T(8,128)S(1)}, u32[]{:S(2)}) copy-start(f32[512,32]{0,1:T(8,128)S(1)} %get-tuple-element.77) | copy-start | bytes 196612
  12.0 96.3 %copy-start.2 = (bf16[512,12,64]{2,0,1:T(8,128)(2,1)}, bf16[512,12,64]{2,0,1:T(8,128)(2,1)S(1)}, u32[]{:S(2)}) copy-start(bf16[512,12,64]{2,0,1:T(8,128)(2,1)S(1)} %broadcast_in_dim.27) | copy-start | bytes 2359300
  95.5 4.7 %copy-start.22 = (bf16[512,768]{1,0:T(8,128)(2,1)S(1)}, bf16[512,768]{1,0:T(8,128)(2,1)}, u32[]{:S(2)}) copy-start(bf16[512,768]{1,0:T(8,128)(2,1)} %param.12) | copy-start | bytes 2359300
  102.4 3.5 copy-start.20
  105.8 4.3 %copy-start = (bf16[512,12,64]{2,0,1:T(8,128)(2,1)}, bf16[512,12,64]{2,0,1:T(8,128)(2,1)S(1)}, u32[]{:S(2)}) copy-start(bf16[512,12,64]{2,0,1:T(8,128)(2,1)S(1)} %copy.44) | copy-start | bytes 2359300
  110.1 9.0 %copy-start.18 = (bf16[1,512,4,192]{1,3,0,2:T(8,128)(2,1)S(1)}, bf16[1,512,4,192]{1,3,0,2:T(8,128)(2,1)}, u32[]{:S(2)}) copy-start(bf16[1,512,4,192]{1,3,0,2:T(8,128)(2,1)} %get-tuple-element.68) | copy-start | bytes 2359300
  119.1 8.3 %slice-start.5 = ((s8[4718592]{0:T(1024)(128)(4,1)}), s8[4194304]{0:T(1024)(128)(4,1)S(1)}, s32[]{:S(2)}) async-start(s8[4718592]{0:T(1024)(128)(4,1)} %bitcast.203), calls=%async_computation.5 | async-start | bytes 8388608
  119.1 6.0 %copy-start.10 = (bf16[4,192,768]{2,1,0:T(8,128)(2,1)S(1)}, bf16[4,192,768]{2,1,0:T(8,128)(2,1)}, u32[]{:S(2)}) copy-start(bf16[4,192,768]{2,1,0:T(8,128)(2,1)} %slice.119) | copy-start | bytes 3538948
  119.1 6.0 %copy-start.23 = (bf16[512,768]{1,0:T(8,128)(2,1)S(1)}, bf16[512,768]{1,0:T(8,128)(2,1)}, u32[]{:S(2)}) copy-start(bf16[512,768]{1,0:T(8,128)(2,1)} %param.12) | copy-start | bytes 2359300
  119.1 8.3 %slice-start.6 = ((s8[4718592]{0:T(1024)(128)(4,1)}), s8[524288]{0:T(1024)(128)(4,1)S(1)}, s32[]{:S(2)}) async-start(s8[4718592]{0:T(1024)(128)(4,1)} %bitcast.203), calls=%async_computation.6 | async-start | bytes 1048576
  125.1 21.8 %copy-start.25 = (bf16[12,64,512]{2,1,0:T(8,128)(2,1)}, bf16[12,64,512]{2,1,0:T(8,128)(2,1)S(1)}, u32[]{:S(2)}) copy-start(bf16[12,64,512]{2,1,0:T(8,128)(2,1)S(1)} %fusion.54) | copy-start | bytes 2359300
  127.1 24.7 %copy-start.4 = (f32[512,768]{1,0:T(8,128)}, f32[512,768]{1,0:T(8,128)S(1)}, u32[]{:S(2)}) copy-start(f32[512,768]{1,0:T(8,128)S(1)} %get-tuple-element.65) | copy-start | bytes 4718596
  151.8 10.2 %copy-start.13 = (bf16[512,768]{1,0:T(8,128)(2,1)S(1)}, bf16[512,768]{1,0:T(8,128)(2,1)}, u32[]{:S(2)}) copy-start(bf16[512,768]{1,0:T(8,128)(2,1)} %param.23) | copy-start | bytes 2359300
  199.4 21.1 %slice-start = ((s8[6291456]{0:T(1024)(128)(4,1)}), s8[2097152]{0:T(1024)(128)(4,1)S(1)}, s32[]{:S(2)}) async-start(s8[6291456]{0:T(1024)(128)(4,1)} %bitcast.158), calls=%async_computation | async-start | bytes 4194304
  206.6 13.9 %slice-start.1 = ((s8[6291456]{0:T(1024)(128)(4,1)}), s8[4194304]{0:T(1024)(128)(4,1)S(1)}, s32[]{:S(2)}) async-start(s8[6291456]{0:T(1024)(128)(4,1)} %bitcast.158), calls=%async_computation.1 | async-start | bytes 8388608
  206.6 13.9 %copy-start.9 = (f32[512,768]{1,0:T(8,128)S(1)}, f32[512,768]{1,0:T(8,128)}, u32[]{:S(2)}) copy-start(f32[512,768]{1,0:T(8,128)} %get-tuple-element.58) | copy-start | bytes 4718596
  220.5 8.5 %copy-start.5 = (f32[512,768]{1,0:T(8,128)S(1)}, f32[512,768]{1,0:T(8,128)}, u32[]{:S(2)}) copy-start(f32[512,768]{1,0:T(8,128)} %copy-done.4) | copy-start | bytes 4718596
  220.5 8.5 %copy-start.31 = (bf16[512,3072]{1,0:T(8,128)(2,1)S(1)}, bf16[512,3072]{1,0:T(8,128)(2,1)}, u32[]{:S(2)}) copy-start(bf16[512,3072]{1,0:T(8,128)(2,1)} %get-tuple-element.89) | copy-start | bytes 9437188
  229.0 6.6 %copy-start.6 = (f32[512,768]{1,0:T(8,128)S(1)}, f32[512,768]{1,0:T(8,128)}, u32[]{:S(2)}) copy-start(f32[512,768]{1,0:T(8,128)} %copy-done.4) | copy-start | bytes 4718596
  238.0 4.9 %copy-start.14 = (f32[512,768]{1,0:T(8,128)}, f32[512,768]{1,0:T(8,128)S(1)}, u32[]{:S(2)}) copy-start(f32[512,768]{1,0:T(8,128)S(1)} %get-tuple-element.56) | copy-start | bytes 4718596
  247.9 6.7 %copy-start.19 = (bf16[1,512,4,192]{1,3,0,2:T(8,128)(2,1)S(1)}, bf16[1,512,4,192]{1,3,0,2:T(8,128)(2,1)}, u32[]{:S(2)}) copy-start(bf16[1,512,4,192]{1,3,0,2:T(8,128)(2,1)} %get-tuple-element.68) | copy-start | bytes 2359300
  254.6 25.0 %copy-start.33 = (bf16[12,64,512]{2,1,0:T(8,128)(2,1)}, bf16[12,64,512]{2,1,0:T(8,128)(2,1)S(1)}, u32[]{:S(2)}) copy-start(bf16[12,64,512]{2,1,0:T(8,128)(2,1)S(1)} %fusion.57) | copy-start | bytes 2359300
  254.6 10.4 %slice-start.2 = ((s8[12582912]{0:T(1024)(128)(4,1)}), s8[4194304]{0:T(1024)(128)(4,1)S(1)}, s32[]{:S(2)}) async-start(s8[12582912]{0:T(1024)(128)(4,1)} %bitcast.169), calls=%async_computation.2 | async-start | bytes 8388608
  254.7 11.7 %slice-start.3 = ((s8[12582912]{0:T(1024)(128)(4,1)}), s8[4194304]{0:T(1024)(128)(4,1)S(1)}, s32[]{:S(2)}) async-start(s8[12582912]{0:T(1024)(128)(4,1)} %bitcast.169), calls=%async_computation.3 | async-start | bytes 8388608
  254.7 12.9 %slice-start.4 = ((s8[12582912]{0:T(1024)(128)(4,1)}), s8[4194304]{0:T(1024)(128)(4,1)S(1)}, s32[]{:S(2)}) async-start(s8[12582912]{0:T(1024)(128)(4,1)} %bitcast.169), calls=%async_computation.4 | async-start | bytes 8388608
  267.5 7.0 %copy-start.1 = (bf16[512,12,64]{2,0,1:T(8,128)(2,1)S(1)}, bf16[512,12,64]{2,0,1:T(8,128)(2,1)}, u32[]{:S(2)}) copy-start(bf16[512,12,64]{2,0,1:T(8,128)(2,1)} %copy-done) | copy-start | bytes 2359300
  267.5 7.0 %copy-start.3 = (bf16[512,12,64]{2,0,1:T(8,128)(2,1)S(1)}, bf16[512,12,64]{2,0,1:T(8,128)(2,1)}, u32[]{:S(2)}) copy-start(bf16[512,12,64]{2,0,1:T(8,128)(2,1)} %copy-done.2) | copy-start | bytes 2359300
  278.4 2.7 copy-start.15
  281.2 3.9 copy-start.24
  392.5 12.3 %copy-start.17 = (bf16[4,2,96,768]{3,2,1,0:T(8,128)(2,1)S(1)}, bf16[4,2,96,768]{3,2,1,0:T(8,128)(2,1)}, u32[]{:S(2)}) copy-start(bf16[4,2,96,768]{3,2,1,0:T(8,128)(2,1)} %get-tuple-element.28) | copy-start | bytes 3538948
  400.2 6.3 %copy-start.16 = (bf16[4,2,96,768]{3,2,1,0:T(8,128)(2,1)S(1)}, bf16[4,2,96,768]{3,2,1,0:T(8,128)(2,1)}, u32[]{:S(2)}) copy-start(bf16[4,2,96,768]{3,2,1,0:T(8,128)(2,1)} %get-tuple-element.30) | copy-start | bytes 3538948
  (9 other events, 19.4 us)

commit v2 on v0

v2 whole, which is shorter than its diff:
```python
from functools import partial
import math

import jax
import jax.numpy as jnp
from jax import lax
from jax.experimental import pallas as pl
from jax.experimental.pallas import tpu as pltpu
from jax.sharding import PartitionSpec as P

HEAD_DIM = 64
PAGE = 512
FREQ = 16
POS = 64
SPLIT = 8
ROWS_STEP = 64
FF_STEP = 256
REL_LANES = 256

norm_epsilon = 1e-05
score_scale = 0.125
masked_score = -1000000000.0

bf16 = jnp.bfloat16
f32 = jnp.float32
MESH = pl.DeviceIdType.MESH


class Place:
    def __init__(self, dp_size):
        d = lax.axis_index("dp")
        t = lax.axis_index("tensor")
        sub = d % SPLIT
        c = sub % 2
        x = (sub // 2) % 2
        y = sub // 4
        self.t, self.c = t, c
        self.shard = (t, t + 1 - 2 * (t % 2), t + 2 - 4 * (t // 2), 3 - t)
        step_x = (1 - 2 * x) * 2
        step_y = (1 - 2 * y) * 4
        step_1 = (1 - c) * step_x + c * step_y
        step_2 = c * step_x + (1 - c) * step_y
        self.core = {"dp": d + 1 - 2 * c}
        self.one = {"dp": d + step_1}
        self.two = {"dp": d + step_2}
        self.near_z = {"tensor": self.shard[1]}
        self.far_z = {"tensor": self.shard[2]}
        self.yx = sub // 2
        self.yx_1 = (sub + step_1) // 2
        self.yx_2 = (sub + step_2) // 2
        self.yx_12 = (sub + step_1 + step_2) // 2
        self.wide = []
        width = SPLIT
        while width < dp_size:
            self.wide.append({"dp": d + width * (1 - 2 * ((d // width) % 2))})
            width *= 2

    def meet(self):
        barrier = pltpu.get_barrier_semaphore()
        others = [self.core, self.one, self.two, self.near_z, self.far_z, *self.wide]
        for other in others:
            pl.semaphore_signal(barrier, inc=1, device_id=other, device_id_type=MESH)
        pl.semaphore_wait(barrier, len(others))


class Sender:
    def __init__(self):
        self.started = []

    def go(self, source, target, sems, index, device):
        send, recv = sems
        copy = pltpu.make_async_remote_copy(
            src_ref=source,
            dst_ref=target,
            send_sem=send.at[index],
            recv_sem=recv.at[index],
            device_id=device,
            device_id_type=MESH,
        )
        copy.start()
        self.started.append(copy)
        return copy

    def drain(self):
        for copy in self.started:
            copy.wait_send()
        self.started = []


def arrived(copies):
    for copy in copies:
        copy.wait_recv()


class Gather:
    def __init__(self, here, sender, whole, sems, rows):
        self.here, self.sender, self.whole = here, sender, whole
        self.z_sems, self.p_sems = sems
        self.rows = rows
        self.flow = {}

    def spot(self, a, k, yx, c):
        start = pl.multiple_of((yx * 2 + c) * self.rows, self.rows)
        return self.whole[a].at[self.here.shard[k], pl.ds(start, self.rows), :]

    def z_start(self, a):
        here = self.here
        mine = self.spot(a, 0, here.yx, here.c)
        self.flow[a, 1, "z"] = self.sender.go(mine, mine, self.z_sems, (a, 0), here.near_z)
        self.flow[a, 2, "z"] = self.sender.go(mine, mine, self.z_sems, (a, 1), here.far_z)

    def z_relay(self, a):
        here = self.here
        self.flow[a, 1, "z"].wait_recv()
        spot = self.spot(a, 1, here.yx, here.c)
        self.flow[a, 3, "z"] = self.sender.go(spot, spot, self.z_sems, (a, 2), here.far_z)

    def one(self, a, k):
        here = self.here
        if k > 1:
            self.flow[a, k, "z"].wait_recv()
        spot = self.spot(a, k, here.yx, here.c)
        self.flow[a, k, 1] = [self.sender.go(spot, spot, self.p_sems, (a, k, 0), here.one)]

    def two(self, a, k):
        here = self.here
        arrived(self.flow[a, k, 1])
        out = []
        for i, yx in enumerate((here.yx, here.yx_1)):
            spot = self.spot(a, k, yx, here.c)
            out.append(self.sender.go(spot, spot, self.p_sems, (a, k, 1 + i), here.two))
        self.flow[a, k, 2] = out

    def three(self, a, k):
        here = self.here
        arrived(self.flow[a, k, 2])
        out = []
        for i in range(4):
            spot = self.spot(a, k, i, here.c)
            out.append(self.sender.go(spot, spot, self.p_sems, (a, k, 3 + i), here.core))
        self.flow[a, k, 3] = out

    def ready(self, a, k):
        arrived(self.flow[a, k, 3])


class Reduce:
    def __init__(self, here, sender, grads, outs, got, sems, rows):
        self.here, self.sender, self.grads, self.outs = here, sender, grads, outs
        self.got_c, self.got_1, self.got_2, self.got_z, self.got_w = got
        self.g_sems, self.o_sems = sems
        self.rows = rows
        self.flow = {}

    def piece(self, a, yx, c):
        rows = self.rows[a]
        return pl.ds(pl.multiple_of((yx * 2 + c) * rows, rows), rows)

    def spot(self, a, k, yx, c):
        return self.grads[a].at[self.here.shard[k], self.piece(a, yx, c), :]

    def add(self, a, k, yx, other):
        here = self.here
        r = self.piece(a, yx, here.c)
        s = here.shard[k]
        self.grads[a][s, r, :] = self.grads[a][s, r, :] + other

    def c_send(self, a, k):
        here = self.here
        self.flow[a, k, 0] = [
            self.sender.go(
                self.spot(a, k, i, 1 - here.c),
                self.got_c[a].at[k, i],
                self.g_sems,
                (a, k, i),
                here.core,
            )
            for i in range(4)
        ]

    def c_take(self, a, k):
        here = self.here
        arrived(self.flow[a, k, 0])

        def body(i, carry):
            self.add(a, k, i, self.got_c[a][k, i])
            return carry

        lax.fori_loop(0, 4, body, 0)
        self.flow[a, k, 1] = [
            self.sender.go(
                self.spot(a, k, yx, here.c),
                self.got_1[a].at[k, i],
                self.g_sems,
                (a, k, 4 + i),
                here.one,
            )
            for i, yx in ((1, here.yx_12), (0, here.yx_1))
        ]

    def one_take(self, a, k):
        here = self.here
        arrived(self.flow[a, k, 1])
        self.add(a, k, here.yx_2, self.got_1[a][k, 1])
        self.flow[a, k, 2] = [
            self.sender.go(
                self.spot(a, k, here.yx_2, here.c),
                self.got_2[a].at[k],
                self.g_sems,
                (a, k, 6),
                here.two,
            )
        ]
        self.add(a, k, here.yx, self.got_1[a][k, 0])

    def two_take(self, a, k):
        here = self.here
        arrived(self.flow[a, k, 2])
        self.add(a, k, here.yx, self.got_2[a][k])
        spot = self.spot(a, k, here.yx, here.c)
        if k >= 2:
            self.flow[a, k, 3] = [
                self.sender.go(spot, self.got_z[a].at[k - 2], self.g_sems, (a, k, 7), here.far_z)
            ]
        else:
            arrived(self.flow[a, k + 2, 3])
            self.add(a, k, here.yx, self.got_z[a][k])
            if k == 1:
                self.flow[a, k, 3] = [
                    self.sender.go(spot, self.got_z[a].at[2], self.g_sems, (a, k, 7), here.near_z)
                ]

    def z_take(self, a):
        here = self.here
        arrived(self.flow[a, 1, 3])
        self.add(a, 0, here.yx, self.got_z[a][2])
        mine = self.spot(a, 0, here.yx, here.c)
        for i, device in enumerate(here.wide):
            copy = self.sender.go(mine, self.got_w[a].at[i], self.o_sems, (a, 7 + i), device)
            copy.wait_recv()
            copy.wait_send()
            self.sender.started.pop()
            self.add(a, 0, here.yx, self.got_w[a][i])
        r = self.piece(a, here.yx, here.c)
        self.outs[a][r, :] = self.grads[a][here.shard[0], r, :]
        spot = self.outs[a].at[r, :]
        self.flow[a, "o1"] = [self.sender.go(spot, spot, self.o_sems, (a, 0), here.one)]

    def out_two(self, a):
        here = self.here
        arrived(self.flow[a, "o1"])
        out = []
        for i, yx in enumerate((here.yx, here.yx_1)):
            spot = self.outs[a].at[self.piece(a, yx, here.c), :]
            out.append(self.sender.go(spot, spot, self.o_sems, (a, 1 + i), here.two))
        self.flow[a, "o2"] = out

    def out_three(self, a):
        here = self.here
        arrived(self.flow[a, "o2"])
        out = []
        for i in range(4):
            spot = self.outs[a].at[self.piece(a, i, here.c), :]
            out.append(self.sender.go(spot, spot, self.o_sems, (a, 3 + i), here.core))
        self.flow[a, "o3"] = out

    def finish(self, a):
        arrived(self.flow[a, "o3"])


class Totals:
    def __init__(self, here, sender, held, got, sems):
        self.sender, self.held, self.got, self.sems = sender, held, got, sems
        self.ways = [here.core, here.one, here.two, here.near_z, here.far_z, *here.wide]
        self.at = 0

    def start(self):
        i = self.at
        self.copy = self.sender.go(
            self.held.at[i], self.got.at[i], self.sems, (i,), self.ways[i]
        )

    def step(self):
        i = self.at
        self.copy.wait_recv()
        self.held[i + 1] = self.held[i] + self.got[i]
        self.at += 1
        if self.at < len(self.ways):
            self.start()

    def done(self):
        return self.at >= len(self.ways)


def flip(v):
    return jnp.transpose(v)


def mm(a, b):
    return jnp.dot(a, b, preferred_element_type=f32)


def mm_t(a, b):
    return lax.dot_general(a, b, (((1,), (1,)), ((), ())), preferred_element_type=f32)


def attention_forward(s, k, attn, rel, feat, bound, tok_t, q_t, k_t, v_t, probs, att_t, acc, proj):
    part = att_t.shape[1]
    heads = part // HEAD_DIM
    proj[...] = mm(attn[s, 0 : 3 * part, :], tok_t[...]).astype(bf16)
    cos_t, sin_t = feat[0:32, :], feat[32:64, :]
    feat_low = feat[...].astype(bf16)

    def head(h, carry):
        i = k * heads + h
        r0 = pl.multiple_of(h * HEAD_DIM, HEAD_DIM)
        q = proj[pl.ds(r0, HEAD_DIM), :]
        coeffs = lax.dot_general(
            rel[k, pl.ds(r0, HEAD_DIM), :], q, (((0,), (0,)), ((), ())), preferred_element_type=f32
        )
        first, second = coeffs[0:32], coeffs[32:64]
        q_t[i, 0:64, :] = q * score_scale
        q_t[i, 64:96, :] = ((first * sin_t + second * cos_t).astype(bf16)) * score_scale
        q_t[i, 96:128, :] = ((second * sin_t - first * cos_t).astype(bf16)) * score_scale
        k_t[i, 0:64, :] = proj[pl.ds(pl.multiple_of(part + r0, HEAD_DIM), HEAD_DIM), :]
        k_t[i, 64:128, :] = feat_low
        v = proj[pl.ds(pl.multiple_of(2 * part + r0, HEAD_DIM), HEAD_DIM), :]
        v_t[i] = v
        scores = mm(flip(k_t[i]), q_t[i])
        scores = jnp.minimum(scores, jnp.concatenate([bound[...]] * (PAGE // 128), 1))
        top = jnp.max(scores, 0, keepdims=True)
        raised = jnp.exp(scores - top)
        total = jnp.sum(raised, 0, keepdims=True)
        weights = (raised * (1.0 / total)).astype(bf16)
        probs[i] = weights
        att_t[k, pl.ds(r0, HEAD_DIM), :] = mm(v, weights).astype(bf16)
        return carry

    lax.fori_loop(0, heads, head, 0)
    acc[...] += mm(flip(att_t[k]), attn[s, 3 * part : 4 * part, :])


def norm_rows(r, gain, shift):
    average = jnp.mean(r, -1, keepdims=True)
    centred = r - average
    spread = jnp.mean(centred * centred, -1, keepdims=True)
    rstd = lax.rsqrt(spread + norm_epsilon)
    hat = centred * rstd
    return hat, rstd, hat * gain + shift


def norm_rows_back(g, hat, rstd, gain):
    gh = g * gain
    a = jnp.mean(gh, -1, keepdims=True)
    b = jnp.mean(gh * hat, -1, keepdims=True)
    return rstd * (gh - a - hat * b)


def first_norm(tok, acc, hat_one, rstd_one, gains, shifts, live, low, vec):
    vec[8] = jnp.zeros_like(vec[8])
    vec[9] = jnp.zeros_like(vec[9])

    def step(i, carry):
        r = pl.ds(pl.multiple_of(i * ROWS_STEP, ROWS_STEP), ROWS_STEP)
        x = tok[r, :].astype(f32)
        a = acc[r, :]
        hat, rstd, y = norm_rows(x + a, gains[0:1, :], shifts[0:1, :])
        hat_one[r, :] = hat
        rstd_one[r, :] = jnp.broadcast_to(rstd, (ROWS_STEP, 128))
        low[r, :] = y.astype(bf16)
        m = live[r, 0:1]
        vec[8] += jnp.sum(m * x * x, 0, keepdims=True)
        vec[9] += jnp.sum(m * a * a, 0, keepdims=True)
        acc[r, :] = jnp.zeros_like(a)
        return carry

    lax.fori_loop(0, PAGE // ROWS_STEP, step, 0)


def second_norm(acc, hat_one, gains, shifts, live, og, layer_out, grad_low, vec):
    vec[10] = jnp.zeros_like(vec[10])
    vec[1] = jnp.zeros_like(vec[1])
    vec[3] = jnp.zeros_like(vec[3])

    def step(i, carry):
        r = pl.ds(pl.multiple_of(i * ROWS_STEP, ROWS_STEP), ROWS_STEP)
        f = acc[r, :]
        y = hat_one[r, :] * gains[0:1, :] + shifts[0:1, :]
        hat, rstd, out = norm_rows(y + f, gains[1:2, :], shifts[1:2, :])
        layer_out[r, :] = out.astype(bf16)
        m = live[r, 0:1]
        vec[10] += jnp.sum(m * f * f, 0, keepdims=True)
        g = og[r, :].astype(f32)
        vec[1] += jnp.sum(g * hat, 0, keepdims=True)
        vec[3] += jnp.sum(g, 0, keepdims=True)
        back = norm_rows_back(g, hat, rstd, gains[1:2, :])
        acc[r, :] = back
        grad_low[r, :] = back.astype(bf16)
        return carry

    lax.fori_loop(0, PAGE // ROWS_STEP, step, 0)


def first_norm_back(acc, hat_one, rstd_one, gains, grad_low, vec):
    vec[0] = jnp.zeros_like(vec[0])
    vec[2] = jnp.zeros_like(vec[2])

    def step(i, carry):
        r = pl.ds(pl.multiple_of(i * ROWS_STEP, ROWS_STEP), ROWS_STEP)
        g = acc[r, :]
        hat = hat_one[r, :]
        vec[0] += jnp.sum(g * hat, 0, keepdims=True)
        vec[2] += jnp.sum(g, 0, keepdims=True)
        back = norm_rows_back(g, hat, rstd_one[r, 0:1], gains[0:1, :])
        acc[r, :] = back
        grad_low[r, :] = back.astype(bf16)
        return carry

    lax.fori_loop(0, PAGE // ROWS_STEP, step, 0)


def ffn_forward(s, k, w_in, w_out, bias, low, hid_t, slope, hid, acc):
    width = w_in.shape[1]

    def step(j, carry):
        c0 = pl.multiple_of(j * FF_STEP, FF_STEP)
        cols = pl.ds(c0, FF_STEP)
        pre = mm(low[...], w_in[s, :, cols]) + bias[s, :, cols]
        cdf = 0.5 * lax.erf(pre * (2.0**-0.5)) + 0.5
        density = jnp.exp(pre * pre * -0.5) * (1.0 / math.sqrt(2.0 * math.pi))
        slope[k, :, cols] = (cdf + pre * density).astype(bf16)
        act = (pre * cdf).astype(bf16)
        hid[:, cols] = act
        hid_t[k, cols, :] = flip(act)
        return carry

    lax.fori_loop(0, width // FF_STEP, step, 0)
    acc[...] += mm(hid[...], w_out[s])


def ffn_backward(s, k, w_in, w_out, low_t, hid_t, slope, hid, grad_low, acc, vec):
    width = w_in.shape[1]

    def step(j, carry):
        c0 = pl.multiple_of(j * FF_STEP, FF_STEP)
        cols = pl.ds(c0, FF_STEP)
        grad = mm_t(grad_low[...], w_out[s, cols, :])
        pre = (grad * slope[k, :, cols].astype(f32)).astype(bf16)
        hid[:, cols] = pre
        vec[4 + s, :, cols] = jnp.sum(pre.astype(f32), 0, keepdims=True)
        w_out[s, cols, :] = mm(hid_t[k, cols, :], grad_low[...]).astype(bf16)
        return carry

    lax.fori_loop(0, width // FF_STEP, step, 0)
    acc[...] += mm_t(hid[...], w_in[s])
    w_in[s] = mm(low_t[...], hid[...]).astype(bf16)


def attention_backward(s, k, attn, rel, feat, tok, grad_low, grad_low_t, q_t, k_t, v_t, probs, att_t, acc, proj, rel_grad, d_att):
    part = att_t.shape[1]
    heads = part // HEAD_DIM
    d_att[...] = mm(attn[s, 3 * part : 4 * part, :], grad_low_t[...]).astype(bf16)
    attn[s, 3 * part : 4 * part, :] = mm(att_t[k], grad_low[...]).astype(bf16)
    cos_t, sin_t = feat[0:32, :], feat[32:64, :]
    lane = lax.broadcasted_iota(jnp.int32, (HEAD_DIM, 256), 1)
    rel_grad[s] = jnp.zeros((HEAD_DIM, 256), f32)

    def head(h, carry):
        i = k * heads + h
        r0 = pl.multiple_of(h * HEAD_DIM, HEAD_DIM)
        d_out = d_att[pl.ds(r0, HEAD_DIM), :]
        inner = jnp.sum(
            d_out.astype(f32) * att_t[k, pl.ds(r0, HEAD_DIM), :].astype(f32), 0, keepdims=True
        )
        weights = probs[i]
        d_probs = mm(flip(v_t[i]), d_out)
        d_scores = (weights.astype(f32) * (d_probs - inner)).astype(bf16)
        proj[pl.ds(pl.multiple_of(2 * part + r0, HEAD_DIM), HEAD_DIM), :] = mm_t(
            d_out, weights
        ).astype(bf16)
        q_part = q_t[i, 0:64, :]
        proj[pl.ds(pl.multiple_of(part + r0, HEAD_DIM), HEAD_DIM), :] = mm_t(
            q_part, d_scores
        ).astype(bf16)
        d_query = mm(k_t[i], d_scores) * score_scale
        d_turned = d_query[64:128].astype(bf16).astype(f32)
        first, second = d_turned[0:32], d_turned[32:64]
        d_coeffs = jnp.concatenate(
            [first * sin_t - second * cos_t, first * cos_t + second * sin_t], 0
        ).astype(bf16)
        rel_h = rel[k, pl.ds(r0, HEAD_DIM), :]
        proj[pl.ds(r0, HEAD_DIM), :] = (d_query[0:64] + mm(rel_h, d_coeffs)).astype(bf16)
        piece = mm_t(d_coeffs, q_part) * (1.0 / score_scale)
        wide = jnp.concatenate([piece] * 4, 1)
        rel_grad[s] += jnp.where(lane // POS == h, wide, 0.0)
        return carry

    lax.fori_loop(0, heads, head, 0)
    acc[...] += mm(flip(proj[...]), attn[s, 0 : 3 * part, :])
    attn[s, 0 : 3 * part, :] = mm(proj[...], tok[...]).astype(bf16)


def layer_kernel(dp_size, n_wide, *refs):
    it = iter(refs)
    take = lambda n: [next(it) for _ in range(n)]
    tok, qkv_own, rel_own, wo_own, in_own, bias_own, out_own = take(7)
    gains, shifts, lengths, boxes, og = take(5)
    layer_out, tokens_grad = take(2)
    sums = take(4)
    gains_out, shifts_out, bias_out, rms_out = take(4)
    attn, w_in, w_out, rel_t, bias, rel = take(6)
    tok_t, low, low_t, grad_low, grad_low_t = take(5)
    q_t, k_t, v_t, probs, att_t, d_att, proj = take(7)
    acc, hat_one, rstd_one, hid_t, slope, hid, feat, bound, live = take(9)
    rel_grad = next(it)
    got = [take(4) for _ in range(5)]
    held, held_got = take(2)
    local_sem, z_s, z_r, p_s, p_r, m_s, m_r, g_s, g_r, o_s, o_r, t_s, t_r = take(13)

    here = Place(dp_size)
    t = here.t
    shard = here.shard
    part = att_t.shape[1]
    local = [
        pltpu.make_async_copy(source, target, local_sem.at[i])
        for i, (source, target) in enumerate(
            (
                (qkv_own, attn.at[t, 0 : 3 * part, :]),
                (wo_own, attn.at[t, 3 * part : 4 * part, :]),
                (rel_own, rel_t.at[t]),
                (bias_own, bias.at[t]),
                (in_own, w_in.at[t]),
                (out_own, w_out.at[t]),
            )
        )
    ]
    for copy in local:
        copy.start()
    here.meet()
    sender = Sender()
    whole = (attn, w_in, w_out)
    gather = Gather(here, sender, whole, ((z_s, z_r), (p_s, p_r)), attn.shape[1] // SPLIT)
    small = []
    for copy in local[0:4]:
        copy.wait()
    gather.z_start(0)
    for i, every in enumerate((rel_t, bias)):
        spot = every.at[t]
        small.append([sender.go(spot, spot, (m_s, m_r), (i, 0), here.near_z)])
        small[i].append(sender.go(spot, spot, (m_s, m_r), (i, 1), here.far_z))

    tok_t[...] = flip(tok[...])
    acc[...] = jnp.zeros_like(acc)
    page = boxes[:, pl.ds(pl.multiple_of(t * PAGE, PAGE), PAGE)].astype(f32)
    orders = lax.broadcasted_iota(jnp.int32, (FREQ, PAGE), 0).astype(f32)
    rates = 0.5 * jnp.exp(orders * (-math.log(100.0) / FREQ))
    for axis in range(2):
        angles = page[axis : axis + 1, :] * rates
        feat[axis * FREQ : (axis + 1) * FREQ, :] = jnp.cos(angles)
        feat[(axis + 2) * FREQ : (axis + 3) * FREQ, :] = jnp.sin(angles)
    real = lax.broadcasted_iota(jnp.int32, (PAGE, 128), 0) < lengths[t]
    bound[...] = jnp.where(real, 3e38, masked_score)
    live[...] = jnp.where(real, 1.0, 0.0)
    vec = held.at[0]

    gather.z_relay(0)
    for i, every in enumerate((rel_t, bias)):
        arrived(small[i][0:1])
        spot = every.at[shard[1]]
        small[i].append(sender.go(spot, spot, (m_s, m_r), (i, 2), here.far_z))
    for copy in local[4:6]:
        copy.wait()
    gather.z_start(1)

    def attend(k):
        if k > 1:
            arrived(small[0][k - 1 : k])
        rel[k] = flip(rel_t[shard[k]])
        attention_forward(
            shard[k], k, attn, rel, feat, bound, tok_t, q_t, k_t, v_t, probs, att_t, acc, proj
        )

    def feed(k):
        if k > 1:
            arrived(small[1][k - 1 : k])
        ffn_forward(shard[k], k, w_in, w_out, bias, low, hid_t, slope, hid, acc)

    gather.one(0, 1)
    attend(0)
    gather.one(0, 2)
    gather.two(0, 1)
    gather.z_relay(1)
    gather.z_start(2)
    gather.one(1, 1)
    gather.one(0, 3)
    gather.two(0, 2)
    gather.three(0, 1)
    gather.two(0, 3)
    gather.ready(0, 1)
    attend(1)
    gather.two(1, 1)
    gather.three(0, 2)
    gather.one(1, 2)
    gather.ready(0, 2)
    gather.z_relay(2)
    gather.one(2, 1)
    gather.three(0, 3)
    attend(2)
    gather.three(1, 1)
    gather.two(1, 2)
    gather.one(1, 3)
    gather.two(2, 1)
    gather.ready(0, 3)
    attend(3)
    gather.three(1, 2)
    gather.three(2, 1)
    gather.two(1, 3)
    gather.one(2, 2)
    first_norm(tok, acc, hat_one, rstd_one, gains, shifts, live, low, vec)
    feed(0)
    gather.ready(1, 1)
    gather.ready(2, 1)
    gather.two(2, 2)
    gather.one(2, 3)
    gather.three(1, 3)
    low_t[...] = flip(low[...])
    feed(1)
    gather.two(2, 3)
    gather.three(2, 2)
    gather.ready(1, 2)
    gather.ready(2, 2)
    feed(2)
    gather.three(2, 3)
    gather.ready(1, 3)
    gather.ready(2, 3)
    feed(3)
    sender.drain()

    second_norm(acc, hat_one, gains, shifts, live, og, layer_out, grad_low, vec)

    grads = (attn, w_in, w_out, rel_grad)
    rows = [g.shape[1] // SPLIT for g in grads]
    reduce = Reduce(here, sender, grads, sums, got, ((g_s, g_r), (o_s, o_r)), rows)
    totals = Totals(here, sender, held, held_got, (t_s, t_r))

    def feed_back(k):
        ffn_backward(
            shard[k], k, w_in, w_out, low_t, hid_t, slope, hid, grad_low, acc, vec
        )
        reduce.c_send(1, k)
        reduce.c_send(2, k)

    def attend_back(k):
        attention_backward(
            shard[k],
            k,
            attn,
            rel,
            feat,
            tok,
            grad_low,
            grad_low_t,
            q_t,
            k_t,
            v_t,
            probs,
            att_t,
            acc,
            proj,
            rel_grad,
            d_att,
        )
        reduce.c_send(0, k)
        reduce.c_send(3, k)

    def pair(step, k):
        step(1, k)
        step(2, k)

    def heads(step, k):
        step(0, k)
        step(3, k)

    feed_back(3)
    feed_back(2)
    pair(reduce.c_take, 3)
    feed_back(1)
    pair(reduce.c_take, 2)
    pair(reduce.one_take, 3)
    feed_back(0)
    pair(reduce.c_take, 1)
    first_norm_back(acc, hat_one, rstd_one, gains, grad_low, vec)
    grad_low_t[...] = flip(grad_low[...])
    vec[11] = jnp.broadcast_to(jnp.sum(live[:, 0:1], 0, keepdims=True), (1, vec.shape[2]))
    totals.start()
    pair(reduce.two_take, 3)
    pair(reduce.one_take, 2)
    pair(reduce.c_take, 0)
    attend_back(3)
    totals.step()
    pair(reduce.one_take, 1)
    pair(reduce.two_take, 2)
    heads(reduce.c_take, 3)
    attend_back(2)
    totals.step()
    pair(reduce.one_take, 0)
    pair(reduce.two_take, 1)
    heads(reduce.c_take, 2)
    attend_back(1)
    totals.step()
    heads(reduce.one_take, 3)
    pair(reduce.two_take, 0)
    heads(reduce.c_take, 1)
    attend_back(0)
    tokens_grad[...] = acc[...].astype(bf16)
    totals.step()
    reduce.z_take(1)
    reduce.z_take(2)
    heads(reduce.one_take, 2)
    heads(reduce.two_take, 3)
    heads(reduce.c_take, 0)
    totals.step()
    reduce.out_two(1)
    reduce.out_two(2)
    heads(reduce.one_take, 1)
    heads(reduce.two_take, 2)
    reduce.out_three(1)
    reduce.out_three(2)
    heads(reduce.one_take, 0)
    heads(reduce.two_take, 1)
    heads(reduce.two_take, 0)
    heads(lambda a, k: reduce.z_take(a), 0)
    while not totals.done():
        totals.step()
    final = held.at[totals.at]
    for i in range(2):
        gains_out[i : i + 1, :] = final[i]
        shifts_out[i : i + 1, :] = final[2 + i]
    bias_out[...] = final[4 + t]
    count = final[11] * float(gains.shape[1])
    lane = lax.broadcasted_iota(jnp.int32, (1, 128), 1)
    roots = jnp.zeros((1, 128), f32)
    for i in range(3):
        square = jnp.sum(final[8 + i], 1, keepdims=True)
        roots = roots + jnp.where(lane == i, jnp.sqrt(square / count[:, 0:1]), 0.0)
    rms_out[...] = roots
    heads(lambda a, k: reduce.out_two(a), 0)
    reduce.finish(1)
    reduce.finish(2)
    heads(lambda a, k: reduce.out_three(a), 0)
    heads(lambda a, k: reduce.finish(a), 0)
    sender.drain()


def run_layer(dp_size, arrays):
    tok, qkv, rel, wo, w_in, bias, w_out, gains, shifts, lengths, boxes, og = arrays
    rows, width = tok.shape
    part = wo.shape[0]
    units = w_in.shape[1]
    shards = lengths.shape[0]
    heads = shards * (part // HEAD_DIM)
    n_wide = max(0, (dp_size // SPLIT).bit_length() - 1)
    steps = 5 + n_wide
    piece = 4 * part // SPLIT
    vmem = pl.BlockSpec(memory_space=pltpu.VMEM)
    smem = pl.BlockSpec(memory_space=pltpu.SMEM)
    anywhere = pl.BlockSpec(memory_space=pl.ANY)
    dma = pltpu.SemaphoreType.DMA
    V = pltpu.VMEM
    S = jax.ShapeDtypeStruct
    scratch = [
        V((shards, 4 * part, width), bf16),
        V((shards, width, units), bf16),
        V((shards, units, width), bf16),
        V((shards,) + rel.shape, bf16),
        V((shards, 1, units), f32),
        V((shards, part, POS), bf16),
        V((width, rows), bf16),
        V((rows, width), bf16),
        V((width, rows), bf16),
        V((rows, width), bf16),
        V((width, rows), bf16),
        V((heads, HEAD_DIM + POS, rows), bf16),
        V((heads, HEAD_DIM + POS, rows), bf16),
        V((heads, HEAD_DIM, rows), bf16),
        V((heads, rows, rows), bf16),
        V((shards, part, rows), bf16),
        V((part, rows), bf16),
        V((3 * part, rows), bf16),
        V((rows, width), f32),
        V((rows, width), f32),
        V((rows, 128), f32),
        V((shards, units, rows), bf16),
        V((shards, rows, units), bf16),
        V((rows, units), bf16),
        V((POS, rows), f32),
        V((rows, 128), f32),
        V((rows, 128), f32),
        V((shards, POS, REL_LANES), f32),
    ]
    forms = [
        (4 * part // SPLIT, width, bf16),
        (width // SPLIT, units, bf16),
        (units // SPLIT, width, bf16),
        (POS // SPLIT, REL_LANES, f32),
    ]
    for lead in ((4, 4), (4, 2), (4,), (3,), (max(1, n_wide),)):
        scratch += [V(lead + (a, b), kind) for a, b, kind in forms]
    scratch += [V((steps + 1, 12, 1, width), f32), V((steps, 12, 1, width), f32)]
    scratch += [dma((6,))]
    scratch += [dma((3, 3))] * 2
    scratch += [dma((3, 4, 7))] * 2
    scratch += [dma((2, 3))] * 2
    scratch += [dma((4, 4, 8))] * 2
    scratch += [dma((4, 7 + max(1, n_wide)))] * 2
    scratch += [dma((steps,))] * 2
    shapes = [S((rows, width), bf16), S((rows, width), bf16)]
    shapes += [S((SPLIT * a, b), kind) for a, b, kind in forms]
    shapes += [S((2, width), f32), S((2, width), f32), S((1, units), f32), S((1, 128), f32)]
    return pl.pallas_call(
        partial(layer_kernel, dp_size, n_wide),
        out_shape=shapes,
        in_specs=[vmem] + [anywhere] * 6 + [vmem, vmem, smem, vmem, vmem],
        out_specs=[vmem] * len(shapes),
        scratch_shapes=scratch,
        compiler_params=pltpu.CompilerParams(
            collective_id=0, has_side_effects=True, vmem_limit_bytes=67043328
        ),
        name="layer",
    )(*arrays)


def per_device(
    dp_size,
    tokens,
    qkv_weight,
    rel_weight,
    out_weight,
    ffn_in_weight,
    ffn_in_bias,
    ffn_out_weight,
    norm_gains,
    norm_biases,
    page_lengths,
    boxes,
    out_grad,
):
    width = tokens.shape[1]
    part = out_weight.shape[0]
    (
        layer_out,
        tokens_grad,
        attn_sum,
        in_sum,
        out_sum,
        rel_sum,
        gains_grad,
        biases_grad,
        bias_grad,
        roots,
    ) = run_layer(
        dp_size,
        (
            tokens,
            jnp.transpose(qkv_weight, (0, 2, 1)).reshape(3 * part, width),
            jnp.transpose(rel_weight),
            out_weight,
            ffn_in_weight,
            ffn_in_bias.reshape(1, -1),
            ffn_out_weight,
            norm_gains,
            norm_biases,
            page_lengths,
            boxes,
            out_grad,
        ),
    )
    return (
        layer_out,
        tokens_grad,
        jnp.transpose(attn_sum[: 3 * part].reshape(3, part, width), (0, 2, 1)).astype(f32),
        jnp.transpose(rel_sum[:, :part]),
        attn_sum[3 * part :].astype(f32),
        in_sum.astype(f32),
        bias_grad.reshape(-1),
        out_sum.astype(f32),
        gains_grad,
        biases_grad,
        roots[0, :3],
    )


def solution(mesh):
    return jax.shard_map(
        partial(per_device, mesh.shape["dp"]),
        mesh=mesh,
        in_specs=(
            P(("dp", "tensor"), None),
            P(None, None, "tensor"),
            P("tensor", None),
            P("tensor", None),
            P(None, "tensor"),
            P("tensor"),
            P("tensor", None),
            P(),
            P(),
            P("dp"),
            P(None, "dp"),
            P(("dp", "tensor"), None),
        ),
        out_specs=(
            P(("dp", "tensor"), None),
            P(("dp", "tensor"), None),
            P(None, None, "tensor"),
            P("tensor", None),
            P("tensor", None),
            P(None, "tensor"),
            P("tensor"),
            P("tensor", None),
            P(),
            P(),
            P(),
        ),
        check_vma=False,
    )
```

time: 915 us -> 192 us (0.21)
  waiting for transfers between devices: 512 us -> 0 us
  Pallas kernels: 0 us -> 177 us
  local copies, waits for them, and re-layouts: 132 us -> 6.71 us
  matrix products: 125 us -> 0 us
  blocking collectives: 72.1 us -> 0 us
  other arithmetic: 50.8 us -> 6.92 us
  between operations: 15.4 us -> 0.68 us
    all_gather x4 -> x0, waiting for transfers between devices: 253 us -> none  [the longest x1 63.6 us: per_device(): lax.all_gather(grad_two.astype(jnp.bfloat16), 'tensor', axis=0, tiled=True)]
    pallas_call x0 -> x1, Pallas kernels: none -> 177 us  [run_layer(): pl.pallas_call(partial(layer_kernel, dp_size, n_wide), out_shape=shapes,...]
    reduce_scatter x4 -> x0, waiting for transfers between devices: 174 us -> none  [the longest x1 59 us: per_device(): lax.psum_scatter(jnp.dot(lax.slice_in_dim(hidden_low, 0, lax.axis_size('t...]
    dot_general x43 -> x0, matrix products: 125 us -> none  [the longest x1 18.7 us: per_device(): jnp.dot(whole_normed, ffn_in_weight, preferred_element_type=jnp.float32)]
    psum x1 -> x0, waiting for transfers between devices: 83.6 us -> none  [per_device(): lax.psum((qkv_grad, rel_grad, out_weight_grad, ffn_in_grad, ffn_bias_grad...]
    dynamic_update_slice x12 -> x0, local copies, waits for them, and re-layouts: 74 us -> none  [the longest x8 71.2 us: per_device(): lax.map(page_backward, paged + (log_totals, to_pages(grad_attended)))]
    psum x2 -> x0, blocking collectives: 72.1 us -> none  [the longest x1 44.5 us: per_device(): lax.psum((gains_local, shifts_local), ('dp', 'tensor'))]
    reduce_sum x14 -> x0, other arithmetic: 19.2 us -> none  [the longest x2 5.83 us: layer_norm(): return centred * lax.rsqrt(spread + norm_epsilon) * gain + shift]
  transfers between devices with their start and end apart: 9 -> 0, of which waited for: 8 -> 0; matrix products, arithmetic and copies ran while one was open for 3% -> 0% of each run, Pallas kernels for 0% -> 0%
where the time goes in v2:
time: 192 us
  Pallas kernels  177 us (92%)
  other arithmetic  6.92 us (4%)
  local copies, waits for them, and re-layouts  6.71 us (3%)
    pallas_call x1, Pallas kernels, run_layer(): pl.pallas_call(partial(layer_kernel, dp_size, n_wide), out_shape=shapes,...  177 us

profile of v2, /device:TPU:0, one launch (start us, length us, event | category | flops | bytes accessed | tf_op | source)
XLA Modules:
  0.0 191.7 jit_solution(2444579937848798992)
XLA Ops:
  0.6 1.3 reshape.35.refs_5_
  1.9 177.4 %layer.1 = (bf16[512,768]{1,0:T(8,128)(2,1)}, bf16[512,768]{1,0:T(8,128)(2,1)}, bf16[768,768]{1,0:T(8,128)(2,1)}, bf16[768,768]{1,0:T(8,128)(2,1)}, bf16[768,768...) custom-call(bf16[512,768]{1,0:T(8,128)(2,1)} %refs_0_.1, ...), custom_call_target="tpu_custom_call" | custom-call | tf_op jit(solution)/shard_map/layer/pallas_call | solution.py:820
  179.3 1.2 slice.12
  180.6 0.0 copy-start.1
  180.6 1.4 convert_bitcast_fusion
  181.9 1.8 slice_convert_fusion
  183.7 0.0 copy-done.1
  183.7 0.0 copy-start
  183.7 1.6 convert_element_type.22
  185.3 0.1 copy-done
  185.4 0.0 copy-start.4
  185.4 0.0 copy-start.7
  185.4 0.0 copy-start.8
  185.4 0.0 copy-start.3
  185.4 1.6 convert_element_type.23
  187.0 0.0 copy-start.2
  187.0 0.0 copy-done.4
  187.0 0.6 slice_bitcast_fusion
  187.6 0.0 copy-done.7
  187.6 0.6 reduce
  188.2 0.0 copy-done.8
  188.2 0.5 slice_bitcast_fusion.1
  188.8 0.0 copy-done.3
  188.8 0.9 copy.27
  189.6 0.0 copy-done.2
  189.6 0.0 copy-start.6
  189.6 0.0 copy-start.5
  189.6 0.9 copy.28
  190.5 0.0 copy-done.6
  190.5 0.6 copy.29
  191.1 0.0 copy-done.5
  191.1 0.6 copy.30
Async XLA Ops:
  180.6 3.2 %copy-start.1 = (bf16[768,768]{1,0:T(8,128)(2,1)S(1)}, bf16[768,768]{1,0:T(8,128)(2,1)}, u32[]{:S(2)}) copy-start(bf16[768,768]{1,0:T(8,128)(2,1)} %get-tuple-element.25) | copy-start | bytes 3538948
  183.7 1.7 copy-start
  185.4 1.6 copy-start.4
  185.4 2.2 %copy-start.7 = (f32[1,768]{1,0:T(1,128)S(1)}, f32[1,768]{1,0:T(1,128)}, u32[]{:S(2)}) copy-start(f32[1,768]{1,0:T(1,128)} %get-tuple-element.26) | copy-start | bytes 9220
  185.4 2.8 %copy-start.8 = (f32[1,128]{1,0:T(1,128)S(1)}, f32[1,128]{1,0:T(1,128)}, u32[]{:S(2)}) copy-start(f32[1,128]{1,0:T(1,128)} %get-tuple-element.30) | copy-start | bytes 1540
  185.4 3.3 %copy-start.3 = (bf16[512,768]{1,0:T(8,128)(2,1)S(1)}, bf16[512,768]{1,0:T(8,128)(2,1)}, u32[]{:S(2)}) copy-start(bf16[512,768]{1,0:T(8,128)(2,1)} %get-tuple-element.42) | copy-start | bytes 2359300
  187.0 2.6 %copy-start.2 = (bf16[512,768]{1,0:T(8,128)(2,1)S(1)}, bf16[512,768]{1,0:T(8,128)(2,1)}, u32[]{:S(2)}) copy-start(bf16[512,768]{1,0:T(8,128)(2,1)} %get-tuple-element.43) | copy-start | bytes 2359300
  189.6 0.9 copy-start.6
  189.6 1.5 copy-start.5
